TPU v7x, 32 devices: a whole 2x2x4 slice. The times are simulated.
32 devices in a mesh: ccd: 4 (over z), tile: 8 (over y, x, core).
Axes of the slice: x: 2, y: 2, z: 4, core: 2. Of those that a mesh axis runs over, the one named last changes fastest.
Arguments:
- frames: bfloat16 [256, 512, 128], P(None, ('ccd', 'tile')), may hold values from -24 to 24
- source_mask: int32 [256, 512, 128], P(None, ('ccd', 'tile')), may hold values 0 or 1
- good_pixels: int32 [512, 128], P(('ccd', 'tile')), may hold values 0 or 1
Outputs:
- factor: float32 [256, 256], replicated
- basis: bfloat16 [256, 512, 128], P(None, ('ccd', 'tile'))
All inputs are finite; a program needn't handle non-finite values. No bound on the sum of `source_mask` or of `good_pixels` on one device may be relied on, other than what follows from the above.
Results may differ from a plain program's by a relative error of at most 0.00065.
Values may be sent and summed in bfloat16 or wider, within the bound.
A program may use at most 64 MiB of HBM per device.

v0:
```python
import functools
import math

import jax
import jax.numpy as jnp
import numpy as np
from jax import lax
from jax.experimental import pallas as pl
from jax.experimental.pallas import tpu as pltpu
from jax.sharding import PartitionSpec as P

REACH = 16
MESH = pl.DeviceIdType.MESH
HIGH = lax.Precision.HIGHEST
LANES = 128


def column_matrix(tile_cols):
    distance = np.abs(np.arange(tile_cols)[:, None] - np.arange(tile_cols)[None, :])
    norm = np.sum(np.exp(-2.0 * np.abs(np.arange(-REACH, REACH + 1)) / 6.0))
    return np.where(distance <= REACH, np.exp(-distance / 6.0) / norm, 0.0).astype(np.float32)


def matmul(a, b, contract=(1, 0)):
    return lax.dot_general(
        a, b, (((contract[0],), (contract[1],)), ((), ())), precision=HIGH, preferred_element_type=jnp.float32
    )


def factor_block(block, rows_ref):
    groups = LANES // 8
    full = (8, LANES)
    live = [block[8 * g:8 * g + 8, :] for g in range(groups)]
    lane = lax.broadcasted_iota(jnp.int32, full, 1)
    for g in range(groups):
        base = 8 * g
        inside = jnp.logical_and(lane >= base, lane < base + 8)
        cols = [jnp.broadcast_to(live[g][:, base + k:base + k + 1], full) for k in range(8)]
        small = {(j, k): jnp.broadcast_to(cols[k][j:j + 1, :], full) for j in range(8) for k in range(j, 8)}
        rows = []
        for k in range(8):
            row = jnp.broadcast_to(live[g][k:k + 1, :], full)
            rows.append(jnp.where(inside, jnp.where(lane == base + k, 1.0, 0.0), row))
        inv, lower = [], {}
        for j in range(8):
            inv.append(1.0 / small[j, j])
            for k in range(j + 1, 8):
                for m in range(k, 8):
                    small[k, m] = small[k, m] - (small[j, k] * small[j, m]) * inv[j]
            for k in range(j + 1, 8):
                lower[k, j] = small[j, k] * inv[j]
                rows[k] = rows[k] - lower[k, j] * rows[j]
        for j in range(8):
            pivot = small[j, j]
            root = lax.rsqrt(pivot)
            root = root * (1.5 - 0.5 * pivot * root * root)
            out = rows[j]
            for m in range(j, 8):
                out = jnp.where(lane == base + m, small[j, m], out)
            rows_ref[base + j:base + j + 1, :] = (out * root)[:1, :]
        if g == groups - 1:
            break
        back = [rows[k] * inv[k] for k in range(8)]
        for k in range(7, -1, -1):
            for m in range(k):
                back[m] = back[m] - lower[k, m] * back[k]
        for i in range(g + 1, groups):
            total = None
            for k in range(8):
                term = jnp.broadcast_to(live[i][:, base + k:base + k + 1], full) * back[k]
                total = term if total is None else total + term
            live[i] = jnp.where(inside, 0.0, live[i]) - total
    done = rows_ref[...]
    row_id = lax.broadcasted_iota(jnp.int32, (LANES, LANES), 0)
    col_id = lax.broadcasted_iota(jnp.int32, (LANES, LANES), 1)
    upper = jnp.where(col_id >= row_id, done, 0.0)
    inverse = jnp.where(col_id < row_id, done, jnp.where(col_id == row_id, 1.0 / done, 0.0))
    return upper, inverse


def split(value):
    high = value.astype(jnp.bfloat16)
    return high, (value - high.astype(jnp.float32)).astype(jnp.bfloat16)


def product(a, b, contract):
    return lax.dot_general(
        a, b, (((contract[0],), (contract[1],)), ((), ())), preferred_element_type=jnp.float32
    )


def smooth_rows(read, rows):
    decay = math.exp(-1.0 / 6.0)
    tail = math.exp(-(REACH + 1) / 6.0)
    ahead = read(0)
    for p in range(1, REACH + 1):
        ahead = ahead * decay + read(p)
    out = [ahead]
    for i in range(1, rows):
        ahead = ahead * decay + (read(REACH + i) - tail * read(i - 1))
        out.append(ahead)
    last = REACH + rows - 1
    back = read(last + REACH) * decay
    for k in range(REACH - 1, 0, -1):
        back = (back + read(last + k)) * decay
    out[rows - 1] = out[rows - 1] + back
    for i in range(rows - 2, -1, -1):
        p = REACH + i
        back = (back + read(p + 1)) * decay - tail * read(p + REACH + 1)
        out[i] = out[i] + back
    return out


CHUNKS = 8


def exchange_kernel(ccds, tiles, tile_rows, frame_ref, mask_ref, good_ref, w_ref, hi_ref, lo_ref, o_ref, own_ref, halo, pad, done, mine,
                    near, far, whole, hs, hr, s1, r1, s2, r2, s3, r3):
    c, t = lax.axis_index("ccd"), lax.axis_index("tile")
    me, total = c * tiles + t, ccds * tiles
    after, before = lax.rem(me + 1, total), lax.rem(me + total - 1, total)
    after_id = (lax.div(after, tiles), lax.rem(after, tiles))
    before_id = (lax.div(before, tiles), lax.rem(before, tiles))
    barrier = pltpu.get_barrier_semaphore()
    good = good_ref[...].astype(jnp.float32)[None]
    for peer in (before_id, after_id):
        pl.semaphore_signal(barrier, inc=1, device_id=peer, device_id_type=MESH)
    for d in range(1, tiles):
        pl.semaphore_signal(barrier, inc=1, device_id=(c, lax.rem(t + d, tiles)), device_id_type=MESH)
    for d in range(1, ccds):
        pl.semaphore_signal(barrier, inc=1, device_id=(lax.rem(c + d, ccds), t), device_id_type=MESH)
    exposures = hi_ref.shape[0]
    part = exposures // CHUNKS
    span = part * tile_rows
    moves = []
    for k in range(CHUNKS):
        rows = pl.ds(k * span, span)
        block = pl.ds(k * part, part)
        value = frame_ref[block].astype(jnp.float32) * (mask_ref[block].astype(jnp.float32) * good)
        own_ref[rows, :] = value.astype(jnp.bfloat16).reshape(span, LANES)
        if k == 0:
            pl.semaphore_wait(barrier, tiles + ccds)
        pair = []
        for side, peer in enumerate((after_id, before_id)):
            copy = pltpu.make_async_remote_copy(
                src_ref=own_ref.at[rows], dst_ref=halo.at[side, rows], send_sem=hs.at[side, k],
                recv_sem=hr.at[side, k], device_id=peer, device_id_type=MESH)
            copy.start()
            pair.append(copy)
        moves.append(pair)
    has_before = jnp.where(me > 0, 1.0, 0.0)
    has_after = jnp.where(me < total - 1, 1.0, 0.0)
    weights = w_ref[...]
    h = LANES
    for k in range(CHUNKS):
        rows = pl.ds(k * span, span)
        pad[1] = own_ref[rows, :].astype(jnp.float32)
        for copy in moves[k]:
            copy.wait_recv()
        pad[0] = halo[0, rows, :].astype(jnp.float32) * has_before
        pad[2] = halo[1, rows, :].astype(jnp.float32) * has_after
        step = 32

        @pl.loop(0, part // step)
        def _(n):
            def read(p):
                first = n * (step * tile_rows) + p % tile_rows
                return pad[p // tile_rows, pl.ds(first, step, stride=tile_rows), :]

            for r, value in enumerate(smooth_rows(read, tile_rows)):
                done[pl.ds(pl.multiple_of(r * part + n * step, step), step), :] = value

        hi, lo = split(matmul(done[...], weights))
        for r in range(tile_rows):
            hi_ref[k * part:(k + 1) * part, r * h:(r + 1) * h] = hi[r * part:(r + 1) * part]
            lo_ref[k * part:(k + 1) * part, r * h:(r + 1) * h] = lo[r * part:(r + 1) * part]
        if (k + 1) * part == h:
            hi, lo = hi_ref[:h, :], lo_ref[:h, :]
            cross = product(hi, lo, (1, 1))
            first = product(hi, hi, (1, 1)) + product(lo, lo, (1, 1)) + (cross + cross.T)
    hi, lo = hi_ref[h:, :], lo_ref[h:, :]
    rest = product(hi, hi_ref[...], (1, 1)) + product(lo, lo_ref[...], (1, 1)) + (
        product(hi, lo_ref[...], (1, 1)) + product(lo, hi_ref[...], (1, 1)))
    packed = jnp.concatenate([first, rest[:, :h], rest[:, h:]], axis=0)
    share = mine.shape[1]
    for i in range(tiles):
        mine[i] = packed[i * share:(i + 1) * share]
    sent = []
    for d in range(1, tiles):
        peer = lax.rem(t + d, tiles)
        copy = pltpu.make_async_remote_copy(
            src_ref=mine.at[peer], dst_ref=near.at[d - 1], send_sem=s1.at[d - 1], recv_sem=r1.at[d - 1],
            device_id=(c, peer), device_id_type=MESH)
        copy.start()
        sent.append(copy)
    value = mine[t]
    for d in range(1, tiles):
        sent[d - 1].wait_recv()
        value = value + near[d - 1]
    far[c] = value
    second = []
    for d in range(1, ccds):
        copy = pltpu.make_async_remote_copy(
            src_ref=far.at[c], dst_ref=far.at[c], send_sem=s2.at[d - 1], recv_sem=r2.at[d - 1],
            device_id=(lax.rem(c + d, ccds), t), device_id_type=MESH)
        copy.start()
        second.append(copy)
    for copy in second:
        copy.wait_recv()
    value = far[0]
    for i in range(1, ccds):
        value = value + far[i]
    whole[t] = value
    third = []
    for d in range(1, tiles):
        copy = pltpu.make_async_remote_copy(
            src_ref=whole.at[t], dst_ref=whole.at[t], send_sem=s3.at[d - 1], recv_sem=r3.at[d - 1],
            device_id=(c, lax.rem(t + d, tiles)), device_id_type=MESH)
        copy.start()
        third.append(copy)
    for copy in third:
        copy.wait_recv()
    o_ref[...] = whole[...]
    for copy in sum(moves, []) + sent + second + third:
        copy.wait_send()


def exchange(frames, source_mask, good_pixels, weights):
    ccds, tiles = lax.axis_size("ccd"), lax.axis_size("tile")
    exposures, tile_rows, _ = frames.shape
    pixels = tile_rows * LANES
    share = 3 * LANES // tiles
    dma = pltpu.SemaphoreType.DMA
    vm = pl.BlockSpec(memory_space=pltpu.VMEM)
    split_shape = jax.ShapeDtypeStruct((exposures, pixels), jnp.bfloat16)
    span = exposures * tile_rows // CHUNKS
    return pl.pallas_call(
        functools.partial(exchange_kernel, ccds, tiles, tile_rows),
        out_shape=(split_shape, split_shape, jax.ShapeDtypeStruct((tiles, share, LANES), jnp.float32)),
        in_specs=[vm] * 4,
        out_specs=(vm,) * 3,
        scratch_shapes=[
            pltpu.VMEM((exposures * tile_rows, LANES), jnp.bfloat16),
            pltpu.VMEM((2, exposures * tile_rows, LANES), jnp.bfloat16),
            pltpu.VMEM((3, span, LANES), jnp.float32),
            pltpu.VMEM((span, LANES), jnp.float32),
            pltpu.VMEM((tiles, share, LANES), jnp.float32),
            pltpu.VMEM((tiles - 1, share, LANES), jnp.float32),
            pltpu.VMEM((ccds, share, LANES), jnp.float32),
            pltpu.VMEM((tiles, share, LANES), jnp.float32),
            dma((2, CHUNKS)), dma((2, CHUNKS)),
            dma((tiles - 1,)), dma((tiles - 1,)),
            dma((ccds - 1,)), dma((ccds - 1,)),
            dma((tiles - 1,)), dma((tiles - 1,)),
        ],
        compiler_params=pltpu.CompilerParams(collective_id=0, has_side_effects=True),
    )(frames, source_mask, good_pixels, weights)


def solve_kernel(pixel_total, g_ref, hi_ref, lo_ref, f_ref, b_ref, rows_ref, xh_ref, xl_ref, out32):
    h = LANES
    scale = 1.0 / pixel_total
    upper, inv1 = factor_block(g_ref[0] * scale, rows_ref)
    f_ref[:h, :h] = upper
    f_ref[h:, :h] = jnp.zeros((h, h), jnp.float32)
    low = matmul(g_ref[1] * scale, inv1, (1, 1))
    f_ref[:h, h:] = low.T
    rest = g_ref[2] * scale - matmul(low, low, (1, 1))
    upper, inv2 = factor_block(rest, rows_ref)
    f_ref[h:, h:] = upper
    xh_ref[:h, :h], xl_ref[:h, :h] = split(inv1)
    xh_ref[:h, h:] = jnp.zeros((h, h), jnp.bfloat16)
    xl_ref[:h, h:] = jnp.zeros((h, h), jnp.bfloat16)
    xh_ref[h:, h:], xl_ref[h:, h:] = split(inv2)
    xh_ref[h:, :h], xl_ref[h:, :h] = split(-matmul(inv2, matmul(low, inv1)))
    exposures, pixels = hi_ref.shape
    tile_rows = pixels // LANES
    for k in range(tile_rows // 2):
        at = slice(2 * k * LANES, 2 * (k + 1) * LANES)
        hi, lo = hi_ref[:, at], lo_ref[:, at]
        part = product(xh_ref[...], hi, (1, 0)) + (
            product(xh_ref[...], lo, (1, 0)) + product(xl_ref[...], hi, (1, 0)) + product(xl_ref[...], lo, (1, 0)))
        for i in range(2):
            out32[pl.ds(2 * k + i, exposures, stride=tile_rows), :] = part[:, i * LANES:(i + 1) * LANES]
    b_ref[...] = out32[...].astype(jnp.bfloat16)


def solve(gram, hi, lo, pixel_total):
    exposures, pixels = hi.shape
    vm = pl.BlockSpec(memory_space=pltpu.VMEM)
    return pl.pallas_call(
        functools.partial(solve_kernel, pixel_total),
        out_shape=(
            jax.ShapeDtypeStruct((exposures, exposures), jnp.float32),
            jax.ShapeDtypeStruct((exposures * pixels // LANES, LANES), jnp.bfloat16),
        ),
        in_specs=[vm, vm, vm],
        out_specs=(vm, vm),
        scratch_shapes=[
            pltpu.VMEM((LANES, LANES), jnp.float32),
            pltpu.VMEM((exposures, exposures), jnp.bfloat16),
            pltpu.VMEM((exposures, exposures), jnp.bfloat16),
            pltpu.VMEM((exposures * pixels // LANES, LANES), jnp.float32),
        ],
    )(gram, hi, lo)


def per_device(frames, source_mask, good_pixels):
    exposures, tile_rows, tile_cols = frames.shape
    tiles = lax.axis_size("tile")
    pixel_total = float(tile_rows * tile_cols * lax.axis_size("ccd") * tiles)
    hi, lo, summed = exchange(frames, source_mask, good_pixels, column_matrix(tile_cols))
    factor, basis = solve(summed.reshape(3, LANES, LANES), hi, lo, pixel_total)
    return (factor, basis.reshape(exposures, tile_rows, tile_cols))


def solution(mesh):
    in_specs = (
        P(None, ("ccd", "tile"), None),
        P(None, ("ccd", "tile"), None),
        P(("ccd", "tile"), None),
    )
    out_specs = (P(), P(None, ("ccd", "tile"), None))
    return jax.shard_map(
        per_device, mesh=mesh, in_specs=in_specs, out_specs=out_specs, check_vma=False
    )
```

profile of v0, /device:TPU:0, one launch (start us, length us, event | category | flops | bytes accessed | tf_op | source)
XLA Modules:
  0.0 64.6 jit_solution(9733851553925176559)
XLA Ops:
  0.6 48.7 %shard_map.59 = (bf16[256,2048]{1,0:T(8,128)(2,1)}, bf16[256,2048]{1,0:T(8,128)(2,1)}, f32[8,48,128]{2,1,0:T(8,128)}) custom-call(bf16[256,16,128]{2,1,0:T(8,128)(2,1)} %frame_ref.1, s32[256,16,128]{2,1,0:T(8,128)} %mask_ref.1, s32[16,128]{1,0:T(8,128)} %good_ref.1, f32[128,128]{1,0:T(8,128)} %constant.2.clone.w_ref), custom_call_target="tpu_custom_call" | custom-call | tf_op jit(solution)/shard_map/pallas_call | solution.py:237
  49.3 15.3 %shard_map.60 = (f32[256,256]{1,0:T(8,128)}, bf16[4096,128]{1,0:T(8,128)(2,1)}) custom-call(f32[3,128,128]{2,1,0:T(8,128)} %bitcast.2, bf16[256,2048]{1,0:T(8,128)(2,1)} %get-tuple-element.8.hi_ref, bf16[256,2048]{1,0:T(8,128)(2,1)} %get-tuple-element.9.lo_ref), custom_call_target="tpu_custom_call" | custom-call | tf_op jit(solution)/shard_map/pallas_call | solution.py:291
where the time goes:
time: 64.8 us; the launch traced here: 64.6 us
  Pallas kernels  64 us (99%)
    pallas_call x1, Pallas kernels, exchange(): pl.pallas_call(functools.partial(exchange_kernel, ccds, tiles, tile_rows)...  48.7 us
    pallas_call x1, Pallas kernels, solve(): pl.pallas_call(functools.partial(solve_kernel, pixel_total), out_shape=(j...  15.3 us

commit v1 on v0

v1 whole, which is shorter than its diff:
```python
import functools
import math

import jax
import jax.numpy as jnp
import numpy as np
from jax import lax
from jax.experimental import pallas as pl
from jax.experimental.pallas import tpu as pltpu
from jax.sharding import PartitionSpec as P

REACH = 16
MESH = pl.DeviceIdType.MESH
HIGH = lax.Precision.HIGHEST
LANES = 128
CHUNKS = 8
GROUPS = 4
AHEAD = 2
VMEM = 60 << 20


def column_matrix(tile_cols):
    distance = np.abs(np.arange(tile_cols)[:, None] - np.arange(tile_cols)[None, :])
    norm = np.sum(np.exp(-2.0 * np.abs(np.arange(-REACH, REACH + 1)) / 6.0))
    full = np.where(distance <= REACH, np.exp(-distance / 6.0) / norm, 0.0).astype(np.float32)
    high = full.astype(jnp.bfloat16)
    low = (full - high.astype(np.float32)).astype(jnp.bfloat16)
    pair = np.concatenate([high, low], axis=1)
    return np.concatenate([pair, pair], axis=0)


def matmul(a, b, contract=(1, 0)):
    return lax.dot_general(
        a, b, (((contract[0],), (contract[1],)), ((), ())), precision=HIGH, preferred_element_type=jnp.float32
    )


def split(value):
    high = value.astype(jnp.bfloat16)
    return high, (value - high.astype(jnp.float32)).astype(jnp.bfloat16)


def product(a, b, contract):
    return lax.dot_general(
        a, b, (((contract[0],), (contract[1],)), ((), ())), preferred_element_type=jnp.float32
    )


def eliminate(block, offset, rows_ref):
    size = block[0].shape[0]
    groups, wide = size // 8, len(block)
    at, start = divmod(offset, LANES)
    full = (8, LANES)
    live = [[tile[8 * g:8 * g + 8, :] for tile in block] for g in range(groups)]
    lane = lax.broadcasted_iota(jnp.int32, full, 1)
    for g in range(groups):
        base = start + 8 * g
        inside = jnp.logical_and(lane >= base, lane < base + 8)
        cols = [jnp.broadcast_to(live[g][at][:, base + k:base + k + 1], full) for k in range(8)]
        small = {(j, k): jnp.broadcast_to(cols[k][j:j + 1, :], full) for j in range(8) for k in range(j, 8)}
        rows = []
        for k in range(8):
            row = [jnp.broadcast_to(tile[k:k + 1, :], full) for tile in live[g]]
            row[at] = jnp.where(inside, jnp.where(lane == base + k, 1.0, 0.0), row[at])
            rows.append(row)
        inv, lower = [], {}
        for j in range(8):
            inv.append(1.0 / small[j, j])
            for k in range(j + 1, 8):
                for m in range(k, 8):
                    small[k, m] = small[k, m] - (small[j, k] * small[j, m]) * inv[j]
            for k in range(j + 1, 8):
                lower[k, j] = small[j, k] * inv[j]
                rows[k] = [x - lower[k, j] * y for x, y in zip(rows[k], rows[j])]
        for j in range(8):
            pivot = small[j, j]
            root = lax.rsqrt(pivot)
            root = root * (1.5 - 0.5 * pivot * root * root)
            out = list(rows[j])
            for m in range(j, 8):
                out[at] = jnp.where(lane == base + m, small[j, m], out[at])
            for w in range(wide):
                rows_ref[8 * g + j:8 * g + j + 1, w * LANES:(w + 1) * LANES] = (out[w] * root)[:1, :]
        if g == groups - 1:
            break
        back = [[x * inv[k] for x in rows[k]] for k in range(8)]
        for k in range(7, -1, -1):
            for m in range(k):
                back[m] = [x - lower[k, m] * y for x, y in zip(back[m], back[k])]
        for i in range(g + 1, groups):
            total = None
            for k in range(8):
                col = jnp.broadcast_to(live[i][at][:, base + k:base + k + 1], full)
                term = [col * y for y in back[k]]
                total = term if total is None else [x + y for x, y in zip(total, term)]
            live[i] = [
                (jnp.where(inside, 0.0, x) if w == at else x) - y for w, (x, y) in enumerate(zip(live[i], total))
            ]


def extend(gram, offset, inverse, lows, rows_ref):
    size = gram[0].shape[0]
    at, start = divmod(offset, LANES)
    wide = at + 1
    shape = (size, LANES)
    lane = lax.broadcasted_iota(jnp.int32, shape, 1)
    row = lax.broadcasted_iota(jnp.int32, shape, 0)
    inside = jnp.logical_and(lane >= start, lane < start + size)
    if offset == 0:
        low = None
        block = [jnp.where(inside, gram[0], 0.0)]
    else:
        value = jnp.concatenate(gram[:wide], axis=1) if wide > 1 else gram[0]
        inv = inverse(wide)
        low = matmul(value, inv, (1, 1))
        lows[offset:offset + size, :wide * LANES] = low
        square = matmul(low, lows[at * LANES:(at + 1) * LANES, :wide * LANES], (1, 1))
        spread = matmul(low, inv)
        block = [-spread[:, w * LANES:(w + 1) * LANES] for w in range(wide)]
        block[at] = jnp.where(inside, gram[at] - square, block[at])
    eliminate(block, offset, rows_ref)
    out, kept = [], []
    for w in range(wide):
        done = rows_ref[:size, w * LANES:(w + 1) * LANES]
        side = None if low is None else low[:, w * LANES:(w + 1) * LANES]
        if w == at:
            upper = jnp.where(lane >= start + row, done, 0.0)
            kept.append(upper if side is None else jnp.where(lane < start, side, upper))
            done = jnp.where(lane < start + row, done, jnp.where(lane == start + row, 1.0 / done, 0.0))
        else:
            kept.append(side)
        out.append(done)
    return out, kept


def smooth_rows(read, rows):
    decay = math.exp(-1.0 / 6.0)
    tail = math.exp(-(REACH + 1) / 6.0)
    ahead = read(0)
    for p in range(1, REACH + 1):
        ahead = ahead * decay + read(p)
    out = [ahead]
    for i in range(1, rows):
        ahead = ahead * decay + (read(REACH + i) - tail * read(i - 1))
        out.append(ahead)
    last = REACH + rows - 1
    back = read(last + REACH) * decay
    for k in range(REACH - 1, 0, -1):
        back = (back + read(last + k)) * decay
    out[rows - 1] = out[rows - 1] + back
    for i in range(rows - 2, -1, -1):
        p = REACH + i
        back = (back + read(p + 1)) * decay - tail * read(p + REACH + 1)
        out[i] = out[i] + back
    return out


def shares(size, tiles, group):
    tall = size * (group * size // LANES + 1)
    return max(8, -(-tall // (8 * tiles)) * 8)


def exchange_kernel(ccds, tiles, pixel_total, frame_hbm, mask_hbm, good_ref, w_ref,
                    hi_hbm, lo_hbm, g_ref, x_ref, f_ref,
                    frames, masks, flat, own, halo, done, hi_ref, lo_ref, lows, rows_ref, *rest):
    bufs = [rest[4 * g:4 * g + 4] for g in range(GROUPS)]
    fs, ms, outs, hs, hr, s1, r1, s2, r2, s3, r3 = rest[4 * GROUPS:]
    exposures, tile_rows, h = frames.shape
    c, t = lax.axis_index("ccd"), lax.axis_index("tile")
    me, total = c * tiles + t, ccds * tiles
    after, before = lax.rem(me + 1, total), lax.rem(me + total - 1, total)
    after_id = (lax.div(after, tiles), lax.rem(after, tiles))
    before_id = (lax.div(before, tiles), lax.rem(before, tiles))
    part = exposures // CHUNKS
    size = exposures // GROUPS
    span = part * tile_rows
    scale = 1.0 / pixel_total
    loads = []
    for k in range(CHUNKS):
        block = pl.ds(k * part, part)
        pair = (pltpu.make_async_copy(frame_hbm.at[block], frames.at[block], fs.at[k]),
                pltpu.make_async_copy(mask_hbm.at[block], masks.at[block], ms.at[k]))
        for copy in pair:
            copy.start()
        loads.append(pair)
    barrier = pltpu.get_barrier_semaphore()
    for peer in (before_id, after_id):
        pl.semaphore_signal(barrier, inc=1, device_id=peer, device_id_type=MESH)
    for d in range(1, tiles):
        pl.semaphore_signal(barrier, inc=1, device_id=(c, lax.rem(t + d, tiles)), device_id_type=MESH)
    for d in range(1, ccds):
        pl.semaphore_signal(barrier, inc=1, device_id=(lax.rem(c + d, ccds), t), device_id_type=MESH)
    good = good_ref[...].astype(jnp.float32)[None]

    def mask(k):
        block = pl.ds(k * part, part)
        for copy in loads[k]:
            copy.wait()
        value = frames[block].astype(jnp.float32) * (masks[block].astype(jnp.float32) * good)
        flat[k % 2] = value.reshape(span, h)
        for r in range(tile_rows):
            own[k, r] = flat[k % 2, pl.ds(r, part, stride=tile_rows), :].astype(jnp.bfloat16)

    moves = []

    def send(k):
        pair = []
        for side, peer in enumerate((after_id, before_id)):
            copy = pltpu.make_async_remote_copy(
                src_ref=own.at[k], dst_ref=halo.at[side, k], send_sem=hs.at[side, k],
                recv_sem=hr.at[side, k], device_id=peer, device_id_type=MESH)
            copy.start()
            pair.append(copy)
        moves.append(pair)

    mask(0)
    pl.semaphore_wait(barrier, tiles + ccds)
    send(0)
    for k in range(1, CHUNKS):
        mask(k)
        if k < AHEAD:
            send(k)
    x_ref[...] = jnp.zeros(x_ref.shape, jnp.float32)
    f_ref[...] = jnp.zeros(f_ref.shape, jnp.float32)
    lows[...] = jnp.zeros(lows.shape, jnp.float32)
    for g in range(GROUPS):
        bufs[g][0][...] = jnp.zeros(bufs[g][0].shape, jnp.float32)
        if (g + 1) * size % LANES and g + 1 < GROUPS:
            for ref in (hi_ref, lo_ref):
                ref[(g + 1) * size:(g + 2) * size, :] = jnp.zeros((size, ref.shape[1]), jnp.bfloat16)
    has_before = jnp.where(me > 0, 1.0, 0.0)
    has_after = jnp.where(me < total - 1, 1.0, 0.0)
    weights = w_ref[...]
    step = 16
    stores = []

    def smooth(k):
        @pl.loop(0, part // step)
        def _(n):
            some = pl.ds(pl.multiple_of(n * step, step), step)

            def read(p):
                if p < tile_rows:
                    return halo[0, k, p, some, :].astype(jnp.float32) * has_before
                if p < 2 * tile_rows:
                    return own[k, p - tile_rows, some, :].astype(jnp.float32)
                return halo[1, k, p - 2 * tile_rows, some, :].astype(jnp.float32) * has_after

            for r, value in enumerate(smooth_rows(read, tile_rows)):
                high, low = split(value)
                where = pl.ds(pl.multiple_of(r * part + n * step, step), step)
                done[where, :h] = high
                done[where, h:] = low

        value = product(done[...], weights, (1, 0))
        high, low = split(value[:, :h] + value[:, h:])
        rows = slice(k * part, (k + 1) * part)
        for r in range(tile_rows):
            hi_ref[rows, r * h:(r + 1) * h] = high[r * part:(r + 1) * part]
            lo_ref[rows, r * h:(r + 1) * h] = low[r * part:(r + 1) * part]
        for i, (src, dst) in enumerate(((hi_ref, hi_hbm), (lo_ref, lo_hbm))):
            copy = pltpu.make_async_copy(src.at[pl.ds(k * part, part)], dst.at[pl.ds(k * part, part)], outs.at[i, k])
            copy.start()
            stores.append(copy)

    sent = []
    waiting = {}

    def launch(g, stage):
        mine, near, far, whole = bufs[g]
        copies = []
        for d in range(1, ccds if stage == 2 else tiles):
            i = d - 1
            if stage == 1:
                peer = lax.rem(t + d, tiles)
                copy = pltpu.make_async_remote_copy(
                    src_ref=mine.at[peer], dst_ref=near.at[i], send_sem=s1.at[g, i], recv_sem=r1.at[g, i],
                    device_id=(c, peer), device_id_type=MESH)
            elif stage == 2:
                copy = pltpu.make_async_remote_copy(
                    src_ref=far.at[c], dst_ref=far.at[c], send_sem=s2.at[g, i], recv_sem=r2.at[g, i],
                    device_id=(lax.rem(c + d, ccds), t), device_id_type=MESH)
            else:
                copy = pltpu.make_async_remote_copy(
                    src_ref=whole.at[t], dst_ref=whole.at[t], send_sem=s3.at[g, i], recv_sem=r3.at[g, i],
                    device_id=(c, lax.rem(t + d, tiles)), device_id_type=MESH)
            copy.start()
            copies.append(copy)
        sent.extend(copies)
        waiting[g] = (stage, copies)

    def gram(g):
        first, stop = g * size, (g + 1) * size
        wide = (first // LANES + 1) * LANES
        some = jnp.concatenate([hi_ref[first:stop, :], lo_ref[first:stop, :]], axis=0)
        value = product(some, hi_ref[:wide, :], (1, 1)) + product(some, lo_ref[:wide, :], (1, 1))
        value = value[:size] + value[size:]
        packed = jnp.concatenate([value[:, w:w + LANES] for w in range(0, wide, LANES)], axis=0)
        mine = bufs[g][0]
        share = mine.shape[1]
        for i in range(packed.shape[0] // share):
            mine[i] = packed[i * share:(i + 1) * share]
        launch(g, 1)

    def advance(g):
        mine, near, far, whole = bufs[g]
        stage, copies = waiting[g]
        for copy in copies:
            copy.wait_recv()
        if stage == 1:
            value = mine[t]
            for d in range(1, tiles):
                value = value + near[d - 1]
            far[c] = value
            launch(g, 2)
        elif stage == 2:
            value = far[0]
            for i in range(1, ccds):
                value = value + far[i]
            whole[t] = value
            launch(g, 3)

    def factor(g):
        whole = bufs[g][3]
        value = whole[...].reshape(-1, LANES) * scale
        tiles_in = [value[w * size:(w + 1) * size] for w in range(g * size // LANES + 1)]
        rows = slice(g * size, (g + 1) * size)
        x, f = extend(tiles_in, g * size, lambda n: x_ref[:n * LANES, :n * LANES], lows, rows_ref)
        for w in range(len(x)):
            x_ref[rows, w * LANES:(w + 1) * LANES] = x[w]
            f_ref[rows, w * LANES:(w + 1) * LANES] = f[w]

    per = CHUNKS // GROUPS
    for k in range(CHUNKS):
        for copy in moves[k]:
            copy.wait_recv()
        if k % per == per - 1:
            for g in range(max(0, k // per - 3), k // per):
                advance(g)
        smooth(k)
        if k % per == per - 1:
            gram(k // per)
        if k + AHEAD < CHUNKS:
            send(k + AHEAD)
    for n in range(3):
        factor(GROUPS - 4 + n)
        for g in range(GROUPS - 1, GROUPS - 4 + n, -1):
            advance(g)
    g_ref[...] = bufs[GROUPS - 1][3][...]
    for copy in stores:
        copy.wait()
    for copy in sum(moves, []) + sent:
        copy.wait_send()


def exchange(frames, source_mask, good_pixels, weights, pixel_total):
    ccds, tiles = lax.axis_size("ccd"), lax.axis_size("tile")
    exposures, tile_rows, _ = frames.shape
    pixels = tile_rows * LANES
    part, size = exposures // CHUNKS, exposures // GROUPS
    span = part * tile_rows
    dma = pltpu.SemaphoreType.DMA
    vm = pl.BlockSpec(memory_space=pltpu.VMEM)
    hbm = pl.BlockSpec(memory_space=pl.ANY)
    split_shape = jax.ShapeDtypeStruct((exposures, pixels), jnp.bfloat16)
    square = jax.ShapeDtypeStruct((exposures, exposures), jnp.float32)
    share = [shares(size, tiles, g) for g in range(GROUPS)]
    reduce = []
    for g in range(GROUPS):
        for n in (tiles, tiles - 1, ccds, tiles):
            reduce.append(pltpu.VMEM((n, share[g], LANES), jnp.float32))
    return pl.pallas_call(
        functools.partial(exchange_kernel, ccds, tiles, pixel_total),
        out_shape=(split_shape, split_shape, jax.ShapeDtypeStruct((tiles, share[-1], LANES), jnp.float32), square, square),
        in_specs=[hbm, hbm, vm, vm],
        out_specs=(hbm, hbm, vm, vm, vm),
        scratch_shapes=[
            pltpu.VMEM(frames.shape, jnp.bfloat16),
            pltpu.VMEM(frames.shape, jnp.int32),
            pltpu.VMEM((2, span, LANES), jnp.float32),
            pltpu.VMEM((CHUNKS, tile_rows, part, LANES), jnp.bfloat16),
            pltpu.VMEM((2, CHUNKS, tile_rows, part, LANES), jnp.bfloat16),
            pltpu.VMEM((span, 2 * LANES), jnp.bfloat16),
            pltpu.VMEM((exposures, pixels), jnp.bfloat16),
            pltpu.VMEM((exposures, pixels), jnp.bfloat16),
            pltpu.VMEM((exposures, exposures), jnp.float32),
            pltpu.VMEM((size, exposures), jnp.float32),
            *reduce,
            dma((CHUNKS,)), dma((CHUNKS,)), dma((2, CHUNKS)),
            dma((2, CHUNKS)), dma((2, CHUNKS)),
            dma((GROUPS, tiles - 1)), dma((GROUPS, tiles - 1)),
            dma((GROUPS, ccds - 1)), dma((GROUPS, ccds - 1)),
            dma((GROUPS, tiles - 1)), dma((GROUPS, tiles - 1)),
        ],
        compiler_params=pltpu.CompilerParams(collective_id=0, has_side_effects=True, vmem_limit_bytes=VMEM),
    )(frames, source_mask, good_pixels, weights)


def solve_kernel(pixel_total, g_ref, x_ref, f_ref, hi_hbm, lo_hbm, o_ref, b_ref,
                 hi_ref, lo_ref, lows, rows_ref, xh_ref, xl_ref, out32, sems):
    loads = (pltpu.make_async_copy(hi_hbm, hi_ref, sems.at[0]), pltpu.make_async_copy(lo_hbm, lo_ref, sems.at[1]))
    for copy in loads:
        copy.start()
    exposures, pixels = hi_ref.shape
    size = exposures // GROUPS
    first = exposures - size
    at = first // LANES
    lows[...] = jnp.zeros(lows.shape, jnp.float32)
    value = g_ref[...].reshape(-1, LANES) * (1.0 / pixel_total)
    block = [value[w * size:(w + 1) * size] for w in range(at + 1)]
    x, f = extend(block, first, lambda n: x_ref[...], lows, rows_ref)
    xh_ref[:first, :], xl_ref[:first, :] = split(x_ref[:first, :])
    xh_ref[first:, :], xl_ref[first:, :] = split(jnp.concatenate(x, axis=1))
    whole = jnp.concatenate([f_ref[:first, :], jnp.concatenate(f, axis=1)], axis=0)
    row = lax.broadcasted_iota(jnp.int32, (exposures, exposures), 0) // size
    col = lax.broadcasted_iota(jnp.int32, (exposures, exposures), 1) // size
    o_ref[...] = jnp.where(row == col, whole, 0.0) + jnp.where(col < row, whole, 0.0).T
    for copy in loads:
        copy.wait()
    tile_rows = pixels // LANES
    for k in range(tile_rows // 2):
        cut = slice(2 * k * LANES, 2 * (k + 1) * LANES)
        hi, lo = hi_ref[:, cut], lo_ref[:, cut]
        part = product(xh_ref[...], hi, (1, 0)) + (
            product(xh_ref[...], lo, (1, 0)) + product(xl_ref[...], hi, (1, 0)) + product(xl_ref[...], lo, (1, 0)))
        for i in range(2):
            out32[pl.ds(2 * k + i, exposures, stride=tile_rows), :] = part[:, i * LANES:(i + 1) * LANES]
    b_ref[...] = out32[...].astype(jnp.bfloat16)


def solve(gram, x, f, hi, lo, pixel_total):
    exposures, pixels = hi.shape
    vm = pl.BlockSpec(memory_space=pltpu.VMEM)
    hbm = pl.BlockSpec(memory_space=pl.ANY)
    square = (exposures, exposures)
    return pl.pallas_call(
        functools.partial(solve_kernel, pixel_total),
        out_shape=(
            jax.ShapeDtypeStruct(square, jnp.float32),
            jax.ShapeDtypeStruct((exposures * pixels // LANES, LANES), jnp.bfloat16),
        ),
        in_specs=[vm, vm, vm, hbm, hbm],
        out_specs=(vm, vm),
        scratch_shapes=[
            pltpu.VMEM((exposures, pixels), jnp.bfloat16),
            pltpu.VMEM((exposures, pixels), jnp.bfloat16),
            pltpu.VMEM(square, jnp.float32),
            pltpu.VMEM((exposures // GROUPS, exposures), jnp.float32),
            pltpu.VMEM(square, jnp.bfloat16),
            pltpu.VMEM(square, jnp.bfloat16),
            pltpu.VMEM((exposures * pixels // LANES, LANES), jnp.float32),
            pltpu.SemaphoreType.DMA((2,)),
        ],
        compiler_params=pltpu.CompilerParams(vmem_limit_bytes=VMEM),
    )(gram, x, f, hi, lo)


def per_device(frames, source_mask, good_pixels):
    exposures, tile_rows, tile_cols = frames.shape
    tiles = lax.axis_size("tile")
    pixel_total = float(tile_rows * tile_cols * lax.axis_size("ccd") * tiles)
    hi, lo, gram, x, f = exchange(frames, source_mask, good_pixels, column_matrix(tile_cols), pixel_total)
    factor, basis = solve(gram, x, f, hi, lo, pixel_total)
    return (factor, basis.reshape(exposures, tile_rows, tile_cols))


def solution(mesh):
    in_specs = (
        P(None, ("ccd", "tile"), None),
        P(None, ("ccd", "tile"), None),
        P(("ccd", "tile"), None),
    )
    out_specs = (P(), P(None, ("ccd", "tile"), None))
    return jax.shard_map(
        per_device, mesh=mesh, in_specs=in_specs, out_specs=out_specs, check_vma=False
    )
```

time: 64.8 us -> 58.5 us (0.903)
  Pallas kernels: 64 us -> 57.5 us
    pallas_call x1, Pallas kernels: 15.3 us -> 8.43 us  [solve(): pl.pallas_call(functools.partial(solve_kernel, pixel_total), out_shape=(j...]
where the time goes in v1:
time: 58.5 us; the launch traced here: 58.3 us
  Pallas kernels  57.5 us (98%)
  between operations  0.8 us (1%)
    pallas_call x1, Pallas kernels, exchange(): pl.pallas_call(functools.partial(exchange_kernel, ccds, tiles, pixel_tota...  49.1 us
    pallas_call x1, Pallas kernels, solve(): pl.pallas_call(functools.partial(solve_kernel, pixel_total), out_shape=(j...  8.43 us

profile of v1, /device:TPU:0, one launch (start us, length us, event | category | flops | bytes accessed | tf_op | source)
XLA Modules:
  0.0 58.3 jit_solution(15870793013091629384)
XLA Ops:
  0.6 49.1 %shard_map.59 = (bf16[256,2048]{1,0:T(8,128)(2,1)}, bf16[256,2048]{1,0:T(8,128)(2,1)}, f32[8,16,128]{2,1,0:T(8,128)}, f32[256,256]{1,0:T(8,128)}, f32[256,256]{1,0:T(8,128)}) custom-call(bf16[256,16,128]{2,1,0:T(8,128)(2,1)} %frame_hbm.1, s32[256,16,128]{2,1,0:T(8,128)} %mask_hbm.1, s32[16,128]{1,0:T(8,128)} %good_ref.1, bf16[256,256]{1,0:T(8,128)(2,1)} %constant.2.clone.w_ref), custom_call_target="tpu_custom_call" | custom-call | tf_op jit(solution)/shard_map/pallas_call | solution.py:372
  49.7 8.4 %shard_map.60 = (f32[256,256]{1,0:T(8,128)}, bf16[4096,128]{1,0:T(8,128)(2,1)}) custom-call(f32[8,16,128]{2,1,0:T(8,128)} %get-tuple-element.9.g_ref, f32[256,256]{1,0:T(8,128)} %get-tuple-element.10.x_ref, f32[256,256]{1,0:T(8,128)} %get-tuple-element.11.f_ref, bf16[256,2048]{1,0:T(8,128)(2,1)} %get-tuple-element.12.hi_hbm, ...), custom_call_target="tpu_custom_call" | custom-call | tf_op jit(solution)/shard_map/pallas_call | solution.py:436

commit v2 on v1

--- a/solution.py
+++ b/solution.py
@@ -16,7 +16,7 @@
 CHUNKS = 8
 GROUPS = 4
 AHEAD = 2
-VMEM = 60 << 20
+VMEM = 40 << 20
 
 
 def column_matrix(tile_cols):
@@ -160,11 +160,11 @@
     return max(8, -(-tall // (8 * tiles)) * 8)
 
 
-def exchange_kernel(ccds, tiles, pixel_total, frame_hbm, mask_hbm, good_ref, w_ref,
-                    hi_hbm, lo_hbm, g_ref, x_ref, f_ref,
-                    frames, masks, flat, own, halo, done, hi_ref, lo_ref, lows, rows_ref, *rest):
+def exchange_kernel(ccds, tiles, pixel_total, frame_hbm, mask_hbm, good_hbm, w_hbm,
+                    hi_ref, lo_ref, g_ref, x_ref, f_ref,
+                    good_ref, w_ref, frames, masks, flat, own, halo, done, lows, rows_ref, *rest):
     bufs = [rest[4 * g:4 * g + 4] for g in range(GROUPS)]
-    fs, ms, outs, hs, hr, s1, r1, s2, r2, s3, r3 = rest[4 * GROUPS:]
+    fs, ms, ws, hs, hr, s1, r1, s2, r2, s3, r3 = rest[4 * GROUPS:]
     exposures, tile_rows, h = frames.shape
     c, t = lax.axis_index("ccd"), lax.axis_index("tile")
     me, total = c * tiles + t, ccds * tiles
@@ -176,6 +176,8 @@
     span = part * tile_rows
     scale = 1.0 / pixel_total
     loads = []
+    small = [pltpu.make_async_copy(good_hbm, good_ref, ws.at[0]), pltpu.make_async_copy(w_hbm, w_ref, ws.at[1])]
+    small[0].start()
     for k in range(CHUNKS):
         block = pl.ds(k * part, part)
         pair = (pltpu.make_async_copy(frame_hbm.at[block], frames.at[block], fs.at[k]),
@@ -183,6 +185,7 @@
         for copy in pair:
             copy.start()
         loads.append(pair)
+    small[1].start()
     barrier = pltpu.get_barrier_semaphore()
     for peer in (before_id, after_id):
         pl.semaphore_signal(barrier, inc=1, device_id=peer, device_id_type=MESH)
@@ -190,6 +193,7 @@
         pl.semaphore_signal(barrier, inc=1, device_id=(c, lax.rem(t + d, tiles)), device_id_type=MESH)
     for d in range(1, ccds):
         pl.semaphore_signal(barrier, inc=1, device_id=(lax.rem(c + d, ccds), t), device_id_type=MESH)
+    small[0].wait()
     good = good_ref[...].astype(jnp.float32)[None]
 
     def mask(k):
@@ -230,9 +234,9 @@
                 ref[(g + 1) * size:(g + 2) * size, :] = jnp.zeros((size, ref.shape[1]), jnp.bfloat16)
     has_before = jnp.where(me > 0, 1.0, 0.0)
     has_after = jnp.where(me < total - 1, 1.0, 0.0)
+    small[1].wait()
     weights = w_ref[...]
     step = 16
-    stores = []
 
     def smooth(k):
         @pl.loop(0, part // step)
@@ -258,10 +262,6 @@
         for r in range(tile_rows):
             hi_ref[rows, r * h:(r + 1) * h] = high[r * part:(r + 1) * part]
             lo_ref[rows, r * h:(r + 1) * h] = low[r * part:(r + 1) * part]
-        for i, (src, dst) in enumerate(((hi_ref, hi_hbm), (lo_ref, lo_hbm))):
-            copy = pltpu.make_async_copy(src.at[pl.ds(k * part, part)], dst.at[pl.ds(k * part, part)], outs.at[i, k])
-            copy.start()
-            stores.append(copy)
 
     sent = []
     waiting = {}
@@ -347,8 +347,6 @@
         for g in range(GROUPS - 1, GROUPS - 4 + n, -1):
             advance(g)
     g_ref[...] = bufs[GROUPS - 1][3][...]
-    for copy in stores:
-        copy.wait()
     for copy in sum(moves, []) + sent:
         copy.wait_send()
 
@@ -362,8 +360,8 @@
     dma = pltpu.SemaphoreType.DMA
     vm = pl.BlockSpec(memory_space=pltpu.VMEM)
     hbm = pl.BlockSpec(memory_space=pl.ANY)
-    split_shape = jax.ShapeDtypeStruct((exposures, pixels), jnp.bfloat16)
-    square = jax.ShapeDtypeStruct((exposures, exposures), jnp.float32)
+    split_shape = pltpu.VMEM((exposures, pixels), jnp.bfloat16)
+    square = pltpu.VMEM((exposures, exposures), jnp.float32)
     share = [shares(size, tiles, g) for g in range(GROUPS)]
     reduce = []
     for g in range(GROUPS):
@@ -371,88 +369,89 @@
             reduce.append(pltpu.VMEM((n, share[g], LANES), jnp.float32))
     return pl.pallas_call(
         functools.partial(exchange_kernel, ccds, tiles, pixel_total),
-        out_shape=(split_shape, split_shape, jax.ShapeDtypeStruct((tiles, share[-1], LANES), jnp.float32), square, square),
-        in_specs=[hbm, hbm, vm, vm],
-        out_specs=(hbm, hbm, vm, vm, vm),
+        out_shape=(split_shape, split_shape, pltpu.VMEM((tiles, share[-1], LANES), jnp.float32), square, square),
+        in_specs=[hbm] * 4,
+        out_specs=(vm,) * 5,
         scratch_shapes=[
+            pltpu.VMEM(good_pixels.shape, jnp.int32),
+            pltpu.VMEM(weights.shape, jnp.bfloat16),
             pltpu.VMEM(frames.shape, jnp.bfloat16),
             pltpu.VMEM(frames.shape, jnp.int32),
             pltpu.VMEM((2, span, LANES), jnp.float32),
             pltpu.VMEM((CHUNKS, tile_rows, part, LANES), jnp.bfloat16),
             pltpu.VMEM((2, CHUNKS, tile_rows, part, LANES), jnp.bfloat16),
             pltpu.VMEM((span, 2 * LANES), jnp.bfloat16),
-            pltpu.VMEM((exposures, pixels), jnp.bfloat16),
-            pltpu.VMEM((exposures, pixels), jnp.bfloat16),
             pltpu.VMEM((exposures, exposures), jnp.float32),
             pltpu.VMEM((size, exposures), jnp.float32),
             *reduce,
-            dma((CHUNKS,)), dma((CHUNKS,)), dma((2, CHUNKS)),
+            dma((CHUNKS,)), dma((CHUNKS,)), dma((2,)),
             dma((2, CHUNKS)), dma((2, CHUNKS)),
             dma((GROUPS, tiles - 1)), dma((GROUPS, tiles - 1)),
             dma((GROUPS, ccds - 1)), dma((GROUPS, ccds - 1)),
             dma((GROUPS, tiles - 1)), dma((GROUPS, tiles - 1)),
         ],
         compiler_params=pltpu.CompilerParams(collective_id=0, has_side_effects=True, vmem_limit_bytes=VMEM),
-    )(frames, source_mask, good_pixels, weights)
-
-
-def solve_kernel(pixel_total, g_ref, x_ref, f_ref, hi_hbm, lo_hbm, o_ref, b_ref,
-                 hi_ref, lo_ref, lows, rows_ref, xh_ref, xl_ref, out32, sems):
-    loads = (pltpu.make_async_copy(hi_hbm, hi_ref, sems.at[0]), pltpu.make_async_copy(lo_hbm, lo_ref, sems.at[1]))
-    for copy in loads:
-        copy.start()
+    )(*(pltpu.with_memory_space_constraint(x, pltpu.HBM) for x in (frames, source_mask, good_pixels, weights)))
+
+
+def solve_kernel(pixel_total, g_ref, x_ref, f_ref, hi_ref, lo_ref, o_ref, b_hbm,
+                 lows, rows_ref, out32, packed, sems):
     exposures, pixels = hi_ref.shape
+    tile_rows = pixels // LANES
     size = exposures // GROUPS
     first = exposures - size
     at = first // LANES
+    copies = []
+
+    def basis(start, x):
+        tall = x.shape[0]
+        both = jnp.concatenate(split(x), axis=0)
+        for k in range(tile_rows // 2):
+            cut = slice(2 * k * LANES, 2 * (k + 1) * LANES)
+            value = product(both, hi_ref[:, cut], (1, 0)) + product(both, lo_ref[:, cut], (1, 0))
+            value = value[:tall] + value[tall:]
+            for i in range(2):
+                out32[pl.ds(start * tile_rows + 2 * k + i, tall, stride=tile_rows), :] = value[:, i * LANES:(i + 1) * LANES]
+        rows = pl.ds(start * tile_rows, tall * tile_rows)
+        packed[rows, :] = out32[rows, :].astype(jnp.bfloat16)
+        copy = pltpu.make_async_copy(packed.at[rows], b_hbm.at[rows], sems.at[len(copies)])
+        copy.start()
+        copies.append(copy)
+
+    basis(0, x_ref[:first, :])
     lows[...] = jnp.zeros(lows.shape, jnp.float32)
     value = g_ref[...].reshape(-1, LANES) * (1.0 / pixel_total)
     block = [value[w * size:(w + 1) * size] for w in range(at + 1)]
     x, f = extend(block, first, lambda n: x_ref[...], lows, rows_ref)
-    xh_ref[:first, :], xl_ref[:first, :] = split(x_ref[:first, :])
-    xh_ref[first:, :], xl_ref[first:, :] = split(jnp.concatenate(x, axis=1))
+    basis(first, jnp.concatenate(x, axis=1))
     whole = jnp.concatenate([f_ref[:first, :], jnp.concatenate(f, axis=1)], axis=0)
     row = lax.broadcasted_iota(jnp.int32, (exposures, exposures), 0) // size
     col = lax.broadcasted_iota(jnp.int32, (exposures, exposures), 1) // size
     o_ref[...] = jnp.where(row == col, whole, 0.0) + jnp.where(col < row, whole, 0.0).T
-    for copy in loads:
+    for copy in copies:
         copy.wait()
-    tile_rows = pixels // LANES
-    for k in range(tile_rows // 2):
-        cut = slice(2 * k * LANES, 2 * (k + 1) * LANES)
-        hi, lo = hi_ref[:, cut], lo_ref[:, cut]
-        part = product(xh_ref[...], hi, (1, 0)) + (
-            product(xh_ref[...], lo, (1, 0)) + product(xl_ref[...], hi, (1, 0)) + product(xl_ref[...], lo, (1, 0)))
-        for i in range(2):
-            out32[pl.ds(2 * k + i, exposures, stride=tile_rows), :] = part[:, i * LANES:(i + 1) * LANES]
-    b_ref[...] = out32[...].astype(jnp.bfloat16)
 
 
 def solve(gram, x, f, hi, lo, pixel_total):
     exposures, pixels = hi.shape
     vm = pl.BlockSpec(memory_space=pltpu.VMEM)
-    hbm = pl.BlockSpec(memory_space=pl.ANY)
     square = (exposures, exposures)
+    rows = (exposures * pixels // LANES, LANES)
+    given = (pltpu.with_memory_space_constraint(value, pltpu.VMEM) for value in (gram, x, f, hi, lo))
     return pl.pallas_call(
         functools.partial(solve_kernel, pixel_total),
-        out_shape=(
-            jax.ShapeDtypeStruct(square, jnp.float32),
-            jax.ShapeDtypeStruct((exposures * pixels // LANES, LANES), jnp.bfloat16),
-        ),
-        in_specs=[vm, vm, vm, hbm, hbm],
-        out_specs=(vm, vm),
+        out_shape=(jax.ShapeDtypeStruct(square, jnp.float32), jax.ShapeDtypeStruct(rows, jnp.bfloat16)),
+        in_specs=[vm] * 5,
+        out_specs=(vm, pl.BlockSpec(memory_space=pl.ANY)),
         scratch_shapes=[
-            pltpu.VMEM((exposures, pixels), jnp.bfloat16),
-            pltpu.VMEM((exposures, pixels), jnp.bfloat16),
             pltpu.VMEM(square, jnp.float32),
             pltpu.VMEM((exposures // GROUPS, exposures), jnp.float32),
-            pltpu.VMEM(square, jnp.bfloat16),
-            pltpu.VMEM(square, jnp.bfloat16),
-            pltpu.VMEM((exposures * pixels // LANES, LANES), jnp.float32),
+            pltpu.VMEM(rows, jnp.float32),
+            pltpu.VMEM(rows, jnp.bfloat16),
             pltpu.SemaphoreType.DMA((2,)),
         ],
         compiler_params=pltpu.CompilerParams(vmem_limit_bytes=VMEM),
-    )(gram, x, f, hi, lo)
+    )(*given)
 
 
 def per_device(frames, source_mask, good_pixels):

time: 58.5 us -> 54 us (0.923)
  Pallas kernels: 57.5 us -> 53.1 us
    pallas_call x1, Pallas kernels: 8.43 us -> 6.18 us  [solve(): pl.pallas_call(functools.partial(solve_kernel, pixel_total), out_shape=(j...]
    pallas_call x1, Pallas kernels: 49.1 us -> 46.9 us  [exchange(): pl.pallas_call(functools.partial(exchange_kernel, ccds, tiles, pixel_tota...]
where the time goes in v2:
time: 54 us; the launch traced here: 53.9 us
  Pallas kernels  53.1 us (98%)
  between operations  0.8 us (1%)
    pallas_call x1, Pallas kernels, exchange(): pl.pallas_call(functools.partial(exchange_kernel, ccds, tiles, pixel_tota...  46.9 us
    pallas_call x1, Pallas kernels, solve(): pl.pallas_call(functools.partial(solve_kernel, pixel_total), out_shape=(j...  6.18 us

profile of v2, /device:TPU:0, one launch (start us, length us, event | category | flops | bytes accessed | tf_op | source)
XLA Modules:
  0.0 53.9 jit_solution(4810071244442225932)
XLA Ops:
  0.6 46.9 %shard_map.59 = (bf16[256,2048]{1,0:T(8,128)(2,1)S(1)}, bf16[256,2048]{1,0:T(8,128)(2,1)S(1)}, f32[8,16,128]{2,1,0:T(8,128)S(1)}, f32[256,256]{1,0:T(8,128)S(1)}, f32[256,256]{1,0:T(8,128)S(1)}) custom-call(bf16[256,16,128]{2,1,0:T(8,128)(2,1)} %frame_hbm.1, s32[256,16,128]{2,1,0:T(8,128)} %mask_hbm.1, s32[16,128]{1,0:T(8,128)} %good_hbm.1, ...), custom_call_target="tpu_custom_call" | custom-call | tf_op jit(solution)/shard_map/pallas_call | solution.py:370
  47.5 6.2 %shard_map.60 = (f32[256,256]{1,0:T(8,128)}, bf16[4096,128]{1,0:T(8,128)(2,1)}) custom-call(f32[8,16,128]{2,1,0:T(8,128)S(1)} %get-tuple-element.9.g_ref, f32[256,256]{1,0:T(8,128)S(1)} %get-tuple-element.10.x_ref, f32[256,256]{1,0:T(8,128)S(1)} %get-tuple-element.11.f_ref, bf16[256,2048]{1,0:T(8,128)(2,1)S(1)} %get-tuple-element.12.hi_ref, ...), custom_call_target="tpu_custom_call" | custom-call | tf_op jit(solution)/shard_map/pallas_call | solution.py:441

commit v3 on v2

--- a/solution.py
+++ b/solution.py
@@ -46,7 +46,7 @@
     )
 
 
-def eliminate(block, offset, rows_ref):
+def eliminate(block, offset, rows_ref, fill=()):
     size = block[0].shape[0]
     groups, wide = size // 8, len(block)
     at, start = divmod(offset, LANES)
@@ -81,6 +81,8 @@
                 out[at] = jnp.where(lane == base + m, small[j, m], out[at])
             for w in range(wide):
                 rows_ref[8 * g + j:8 * g + j + 1, w * LANES:(w + 1) * LANES] = (out[w] * root)[:1, :]
+        for work in fill[g::groups]:
+            work()
         if g == groups - 1:
             break
         back = [[x * inv[k] for x in rows[k]] for k in range(8)]
@@ -98,39 +100,42 @@
             ]
 
 
-def extend(gram, offset, inverse, lows, rows_ref):
+def panel(gram, offset, inv, lows):
     size = gram[0].shape[0]
     at, start = divmod(offset, LANES)
-    wide = at + 1
-    shape = (size, LANES)
-    lane = lax.broadcasted_iota(jnp.int32, shape, 1)
-    row = lax.broadcasted_iota(jnp.int32, shape, 0)
+    lane = lax.broadcasted_iota(jnp.int32, (size, LANES), 1)
     inside = jnp.logical_and(lane >= start, lane < start + size)
     if offset == 0:
-        low = None
-        block = [jnp.where(inside, gram[0], 0.0)]
-    else:
-        value = jnp.concatenate(gram[:wide], axis=1) if wide > 1 else gram[0]
-        inv = inverse(wide)
-        low = matmul(value, inv, (1, 1))
-        lows[offset:offset + size, :wide * LANES] = low
-        square = matmul(low, lows[at * LANES:(at + 1) * LANES, :wide * LANES], (1, 1))
-        spread = matmul(low, inv)
-        block = [-spread[:, w * LANES:(w + 1) * LANES] for w in range(wide)]
-        block[at] = jnp.where(inside, gram[at] - square, block[at])
-    eliminate(block, offset, rows_ref)
-    out, kept = [], []
-    for w in range(wide):
-        done = rows_ref[:size, w * LANES:(w + 1) * LANES]
-        side = None if low is None else low[:, w * LANES:(w + 1) * LANES]
-        if w == at:
-            upper = jnp.where(lane >= start + row, done, 0.0)
-            kept.append(upper if side is None else jnp.where(lane < start, side, upper))
-            done = jnp.where(lane < start + row, done, jnp.where(lane == start + row, 1.0 / done, 0.0))
-        else:
-            kept.append(side)
-        out.append(done)
-    return out, kept
+        return None, None, jnp.where(inside, gram[0], 0.0)
+    value = jnp.concatenate(gram, axis=1) if at else gram[0]
+    low = matmul(value, inv, (1, 1))
+    lows[offset:offset + size, :(at + 1) * LANES] = low
+    square = matmul(low, lows[at * LANES:(at + 1) * LANES, :(at + 1) * LANES], (1, 1))
+    return low, matmul(low, inv), jnp.where(inside, gram[at] - square, 0.0)
+
+
+def triangles(done, start):
+    lane = lax.broadcasted_iota(jnp.int32, done.shape, 1)
+    row = start + lax.broadcasted_iota(jnp.int32, done.shape, 0)
+    upper = jnp.where(lane >= row, done, 0.0)
+    return upper, jnp.where(lane < row, done, jnp.where(lane == row, 1.0 / done, 0.0))
+
+
+def pieces(both, hi_ref, lo_ref, keep):
+    deep, pixels = both.shape[1], hi_ref.shape[1]
+    tall = both.shape[0] // 2
+
+    def piece(at):
+        cut = slice(at, at + 2 * LANES)
+        value = product(both, hi_ref[:deep, cut], (1, 0)) + product(both, lo_ref[:deep, cut], (1, 0))
+        keep(at, value[:tall] + value[tall:])
+
+    return [functools.partial(piece, at) for at in range(0, pixels, 2 * LANES)]
+
+
+def spread_rows(out32, tile_rows, tall, at, value):
+    for i in range(2):
+        out32[pl.ds(at // LANES + i, tall, stride=tile_rows), :] = value[:tall, i * LANES:(i + 1) * LANES]
 
 
 def smooth_rows(read, rows):
@@ -161,8 +166,8 @@
 
 
 def exchange_kernel(ccds, tiles, pixel_total, frame_hbm, mask_hbm, good_hbm, w_hbm,
-                    hi_ref, lo_ref, g_ref, x_ref, f_ref,
-                    good_ref, w_ref, frames, masks, flat, own, halo, done, lows, rows_ref, *rest):
+                    hi_ref, lo_ref, g_ref, x_ref, f_ref, early_ref,
+                    good_ref, w_ref, frames, masks, flat, own, halo, done, lows, rows_ref, out32, *rest):
     bufs = [rest[4 * g:4 * g + 4] for g in range(GROUPS)]
     fs, ms, ws, hs, hr, s1, r1, s2, r2, s3, r3 = rest[4 * GROUPS:]
     exposures, tile_rows, h = frames.shape
@@ -325,10 +330,28 @@
         value = whole[...].reshape(-1, LANES) * scale
         tiles_in = [value[w * size:(w + 1) * size] for w in range(g * size // LANES + 1)]
         rows = slice(g * size, (g + 1) * size)
-        x, f = extend(tiles_in, g * size, lambda n: x_ref[:n * LANES, :n * LANES], lows, rows_ref)
-        for w in range(len(x)):
-            x_ref[rows, w * LANES:(w + 1) * LANES] = x[w]
-            f_ref[rows, w * LANES:(w + 1) * LANES] = f[w]
+        at, start = divmod(g * size, LANES)
+        low, spread, block = panel(tiles_in, g * size, x_ref[:(at + 1) * LANES, :(at + 1) * LANES], lows)
+        lane = lax.broadcasted_iota(jnp.int32, block.shape, 1)
+        live = [block if low is None else jnp.where(lane < start, -spread[:, at * LANES:], block)]
+        if at:
+            live = [-spread[:, w * LANES:(w + 1) * LANES] for w in range(at)] + live
+        fill = []
+        if g:
+            last = slice((g - 1) * size, g * size)
+            deep = ((g - 1) * size // LANES + 1) * LANES
+            both = jnp.concatenate(split(x_ref[last, :deep]), axis=0)
+            fill = pieces(both, hi_ref, lo_ref, functools.partial(spread_rows, out32, tile_rows, size))
+        eliminate(live, g * size, rows_ref, fill)
+        cut = slice(at * LANES, (at + 1) * LANES)
+        upper, lower = triangles(rows_ref[:, cut], start)
+        x_ref[rows, cut] = lower
+        f_ref[rows, cut] = upper if low is None else jnp.where(lane < start, low[:, cut], upper)
+        if at:
+            x_ref[rows, :at * LANES] = rows_ref[:, :at * LANES]
+            f_ref[rows, :at * LANES] = low[:, :at * LANES]
+        if g:
+            early_ref[(g - 1) * size * tile_rows:g * size * tile_rows, :] = out32[...].astype(jnp.bfloat16)
 
     per = CHUNKS // GROUPS
     for k in range(CHUNKS):
@@ -369,9 +392,10 @@
             reduce.append(pltpu.VMEM((n, share[g], LANES), jnp.float32))
     return pl.pallas_call(
         functools.partial(exchange_kernel, ccds, tiles, pixel_total),
-        out_shape=(split_shape, split_shape, pltpu.VMEM((tiles, share[-1], LANES), jnp.float32), square, square),
+        out_shape=(split_shape, split_shape, pltpu.VMEM((tiles, share[-1], LANES), jnp.float32), square, square,
+                   pltpu.VMEM(((GROUPS - 2) * size * tile_rows, LANES), jnp.bfloat16)),
         in_specs=[hbm] * 4,
-        out_specs=(vm,) * 5,
+        out_specs=(vm,) * 6,
         scratch_shapes=[
             pltpu.VMEM(good_pixels.shape, jnp.int32),
             pltpu.VMEM(weights.shape, jnp.bfloat16),
@@ -383,6 +407,7 @@
             pltpu.VMEM((span, 2 * LANES), jnp.bfloat16),
             pltpu.VMEM((exposures, exposures), jnp.float32),
             pltpu.VMEM((size, exposures), jnp.float32),
+            pltpu.VMEM((size * tile_rows, LANES), jnp.float32),
             *reduce,
             dma((CHUNKS,)), dma((CHUNKS,)), dma((2,)),
             dma((2, CHUNKS)), dma((2, CHUNKS)),
@@ -394,61 +419,80 @@
     )(*(pltpu.with_memory_space_constraint(x, pltpu.HBM) for x in (frames, source_mask, good_pixels, weights)))
 
 
-def solve_kernel(pixel_total, g_ref, x_ref, f_ref, hi_ref, lo_ref, o_ref, b_hbm,
-                 lows, rows_ref, out32, packed, sems):
+def solve_kernel(pixel_total, g_ref, x_ref, f_ref, early_ref, hi_ref, lo_ref, o_hbm, b_hbm,
+                 lows, rows_ref, out32, packed, rest_hi, rest_lo, factor, sems):
     exposures, pixels = hi_ref.shape
     tile_rows = pixels // LANES
     size = exposures // GROUPS
+    span = size * tile_rows
     first = exposures - size
-    at = first // LANES
+    at, start = divmod(first, LANES)
     copies = []
 
-    def basis(start, x):
-        tall = x.shape[0]
-        both = jnp.concatenate(split(x), axis=0)
-        for k in range(tile_rows // 2):
-            cut = slice(2 * k * LANES, 2 * (k + 1) * LANES)
-            value = product(both, hi_ref[:, cut], (1, 0)) + product(both, lo_ref[:, cut], (1, 0))
-            value = value[:tall] + value[tall:]
-            for i in range(2):
-                out32[pl.ds(start * tile_rows + 2 * k + i, tall, stride=tile_rows), :] = value[:, i * LANES:(i + 1) * LANES]
-        rows = pl.ds(start * tile_rows, tall * tile_rows)
-        packed[rows, :] = out32[rows, :].astype(jnp.bfloat16)
-        copy = pltpu.make_async_copy(packed.at[rows], b_hbm.at[rows], sems.at[len(copies)])
+    def out(src, dst):
+        copy = pltpu.make_async_copy(src, dst, sems.at[len(copies)])
         copy.start()
         copies.append(copy)
 
-    basis(0, x_ref[:first, :])
+    out(early_ref, b_hbm.at[pl.ds(0, early_ref.shape[0])])
     lows[...] = jnp.zeros(lows.shape, jnp.float32)
     value = g_ref[...].reshape(-1, LANES) * (1.0 / pixel_total)
-    block = [value[w * size:(w + 1) * size] for w in range(at + 1)]
-    x, f = extend(block, first, lambda n: x_ref[...], lows, rows_ref)
-    basis(first, jnp.concatenate(x, axis=1))
-    whole = jnp.concatenate([f_ref[:first, :], jnp.concatenate(f, axis=1)], axis=0)
+    low, spread, block = panel([value[w * size:(w + 1) * size] for w in range(at + 1)], first, x_ref[...], lows)
+    row = first + lax.broadcasted_iota(jnp.int32, (size, exposures), 0)
+    col = lax.broadcasted_iota(jnp.int32, (size, exposures), 1)
+    rest = jnp.where(col < first, -spread, jnp.where(col == row, 1.0, 0.0))
+    xh, xl = split(x_ref[first - size:first, :])
+    rh, rl = split(rest)
+    both = jnp.concatenate([xh, rh, xl, rl], axis=0)
+
+    def keep(cut, value):
+        spread_rows(out32, tile_rows, size, cut, value)
+        high, small = split(value[size:])
+        rest_hi[:, cut:cut + 2 * LANES] = high
+        rest_lo[:, cut:cut + 2 * LANES] = small
+
+    eliminate([block], start, rows_ref, pieces(both, hi_ref, lo_ref, keep))
+    upper, lower = triangles(rows_ref[...], start)
+    packed[:span, :] = out32[...].astype(jnp.bfloat16)
+    out(packed.at[pl.ds(0, span)], b_hbm.at[pl.ds((exposures - 2 * size) * tile_rows, span)])
+    both = jnp.concatenate(split(lower[:, start:start + size]), axis=0)
+    for piece in pieces(both, rest_hi, rest_lo, functools.partial(spread_rows, out32, tile_rows, size)):
+        piece()
+    packed[span:, :] = out32[...].astype(jnp.bfloat16)
+    out(packed.at[pl.ds(span, span)], b_hbm.at[pl.ds(first * tile_rows, span)])
+    whole = jnp.where(col < first, low, jnp.pad(upper, ((0, 0), (at * LANES, 0))) if at else upper)
+    whole = jnp.concatenate([f_ref[:first, :], whole], axis=0)
     row = lax.broadcasted_iota(jnp.int32, (exposures, exposures), 0) // size
     col = lax.broadcasted_iota(jnp.int32, (exposures, exposures), 1) // size
-    o_ref[...] = jnp.where(row == col, whole, 0.0) + jnp.where(col < row, whole, 0.0).T
+    factor[...] = jnp.where(row == col, whole, 0.0) + jnp.where(col < row, whole, 0.0).T
+    out(factor, o_hbm)
     for copy in copies:
         copy.wait()
 
 
-def solve(gram, x, f, hi, lo, pixel_total):
+def solve(gram, x, f, early, hi, lo, pixel_total):
     exposures, pixels = hi.shape
+    size = exposures // GROUPS
+    span = size * pixels // LANES
     vm = pl.BlockSpec(memory_space=pltpu.VMEM)
+    hbm = pl.BlockSpec(memory_space=pl.ANY)
     square = (exposures, exposures)
     rows = (exposures * pixels // LANES, LANES)
-    given = (pltpu.with_memory_space_constraint(value, pltpu.VMEM) for value in (gram, x, f, hi, lo))
+    given = (pltpu.with_memory_space_constraint(value, pltpu.VMEM) for value in (gram, x, f, early, hi, lo))
     return pl.pallas_call(
         functools.partial(solve_kernel, pixel_total),
         out_shape=(jax.ShapeDtypeStruct(square, jnp.float32), jax.ShapeDtypeStruct(rows, jnp.bfloat16)),
-        in_specs=[vm] * 5,
-        out_specs=(vm, pl.BlockSpec(memory_space=pl.ANY)),
+        in_specs=[vm] * 6,
+        out_specs=(hbm, hbm),
         scratch_shapes=[
             pltpu.VMEM(square, jnp.float32),
-            pltpu.VMEM((exposures // GROUPS, exposures), jnp.float32),
-            pltpu.VMEM(rows, jnp.float32),
-            pltpu.VMEM(rows, jnp.bfloat16),
-            pltpu.SemaphoreType.DMA((2,)),
+            pltpu.VMEM((size, LANES), jnp.float32),
+            pltpu.VMEM((span, LANES), jnp.float32),
+            pltpu.VMEM((2 * span, LANES), jnp.bfloat16),
+            pltpu.VMEM((size, pixels), jnp.bfloat16),
+            pltpu.VMEM((size, pixels), jnp.bfloat16),
+            pltpu.VMEM(square, jnp.float32),
+            pltpu.SemaphoreType.DMA((4,)),
         ],
         compiler_params=pltpu.CompilerParams(vmem_limit_bytes=VMEM),
     )(*given)
@@ -458,8 +502,8 @@
     exposures, tile_rows, tile_cols = frames.shape
     tiles = lax.axis_size("tile")
     pixel_total = float(tile_rows * tile_cols * lax.axis_size("ccd") * tiles)
-    hi, lo, gram, x, f = exchange(frames, source_mask, good_pixels, column_matrix(tile_cols), pixel_total)
-    factor, basis = solve(gram, x, f, hi, lo, pixel_total)
+    hi, lo, gram, x, f, early = exchange(frames, source_mask, good_pixels, column_matrix(tile_cols), pixel_total)
+    factor, basis = solve(gram, x, f, early, hi, lo, pixel_total)
     return (factor, basis.reshape(exposures, tile_rows, tile_cols))
 
 

time: 54 us -> 52.3 us (0.969)
  Pallas kernels: 53.1 us -> 51.3 us
    pallas_call x1, Pallas kernels: 6.18 us -> 4.53 us  [solve(): pl.pallas_call(functools.partial(solve_kernel, pixel_total), out_shape=(j...]
where the time goes in v3:
time: 52.3 us; the launch traced here: 52.1 us
  Pallas kernels  51.3 us (98%)
  between operations  0.8 us (2%)
    pallas_call x1, Pallas kernels, exchange(): pl.pallas_call(functools.partial(exchange_kernel, ccds, tiles, pixel_tota...  46.8 us
    pallas_call x1, Pallas kernels, solve(): pl.pallas_call(functools.partial(solve_kernel, pixel_total), out_shape=(j...  4.53 us

profile of v3, /device:TPU:0, one launch (start us, length us, event | category | flops | bytes accessed | tf_op | source)
XLA Modules:
  0.0 52.1 jit_solution(14525830956898667926)
XLA Ops:
  0.6 46.8 %shard_map.59 = (bf16[256,2048]{1,0:T(8,128)(2,1)S(1)}, bf16[256,2048]{1,0:T(8,128)(2,1)S(1)}, f32[8,16,128]{2,1,0:T(8,128)S(1)}, f32[256,256]{1,0:T(8,128)S(1)}...) custom-call(bf16[256,16,128]{2,1,0:T(8,128)(2,1)} %frame_hbm.1, s32[256,16,128]{2,1,0:T(8,128)} %mask_hbm.1, ...), custom_call_target="tpu_custom_call" | custom-call | tf_op jit(solution)/shard_map/pallas_call | solution.py:393
  47.4 4.5 %shard_map.60 = (f32[256,256]{1,0:T(8,128)}, bf16[4096,128]{1,0:T(8,128)(2,1)}) custom-call(f32[8,16,128]{2,1,0:T(8,128)S(1)} %get-tuple-element.10.g_ref, f32[256,256]{1,0:T(8,128)S(1)} %get-tuple-element.11.x_ref, f32[256,256]{1,0:T(8,128)S(1)} %get-tuple-element.12.f_ref, bf16[2048,128]{1,0:T(8,128)(2,1)S(1)} %get-tuple-element.13.early_ref, ...), custom_call_target="tpu_custom_call" | custom-call | tf_op jit(solution)/shard_map/pallas_call | solution.py:482

commit v4 on v3

--- a/solution.py
+++ b/solution.py
@@ -13,9 +13,13 @@
 MESH = pl.DeviceIdType.MESH
 HIGH = lax.Precision.HIGHEST
 LANES = 128
-CHUNKS = 8
-GROUPS = 4
-AHEAD = 2
+CHUNKS = 16
+BOUNDS = (0, 4, 8, 12, 14, 16)
+GROUPS = len(BOUNDS) - 1
+AHEAD = 4
+SLOTS = {8: (0,), 12: (1,), 13: (0,), 15: (2,)}
+FIRST = 13
+TAIL = (((3, 1), 1), ((4, 2), 2), ((3,), 3), ((4,), None))
 VMEM = 40 << 20
 
 
@@ -160,16 +164,22 @@
     return out
 
 
-def shares(size, tiles, group):
-    tall = size * (group * size // LANES + 1)
-    return max(8, -(-tall // (8 * tiles)) * 8)
+def group_rows(exposures, group):
+    part = exposures // CHUNKS
+    return BOUNDS[group] * part, BOUNDS[group + 1] * part
+
+
+def shares(exposures, total, group):
+    first, stop = group_rows(exposures, group)
+    tall = (stop - first) * (first // LANES + 1)
+    return tall, -(-tall // total)
 
 
 def exchange_kernel(ccds, tiles, pixel_total, frame_hbm, mask_hbm, good_hbm, w_hbm,
                     hi_ref, lo_ref, g_ref, x_ref, f_ref, early_ref,
                     good_ref, w_ref, frames, masks, flat, own, halo, done, lows, rows_ref, out32, *rest):
-    bufs = [rest[4 * g:4 * g + 4] for g in range(GROUPS)]
-    fs, ms, ws, hs, hr, s1, r1, s2, r2, s3, r3 = rest[4 * GROUPS:]
+    bufs = [rest[3 * g:3 * g + 3] for g in range(GROUPS)]
+    fs, ms, ws, hs, hr, s1, r1, s2, r2, ready = rest[3 * GROUPS:]
     exposures, tile_rows, h = frames.shape
     c, t = lax.axis_index("ccd"), lax.axis_index("tile")
     me, total = c * tiles + t, ccds * tiles
@@ -177,7 +187,6 @@
     after_id = (lax.div(after, tiles), lax.rem(after, tiles))
     before_id = (lax.div(before, tiles), lax.rem(before, tiles))
     part = exposures // CHUNKS
-    size = exposures // GROUPS
     span = part * tile_rows
     scale = 1.0 / pixel_total
     loads = []
@@ -225,6 +234,8 @@
     mask(0)
     pl.semaphore_wait(barrier, tiles + ccds)
     send(0)
+    for d in range(1, ccds):
+        pl.semaphore_signal(ready, inc=1, device_id=(lax.rem(c + d, ccds), t), device_id_type=MESH)
     for k in range(1, CHUNKS):
         mask(k)
         if k < AHEAD:
@@ -234,9 +245,11 @@
     lows[...] = jnp.zeros(lows.shape, jnp.float32)
     for g in range(GROUPS):
         bufs[g][0][...] = jnp.zeros(bufs[g][0].shape, jnp.float32)
-        if (g + 1) * size % LANES and g + 1 < GROUPS:
+        first, stop = group_rows(exposures, g)
+        left = LANES - stop % LANES
+        if first % LANES == 0 and left < LANES:
             for ref in (hi_ref, lo_ref):
-                ref[(g + 1) * size:(g + 2) * size, :] = jnp.zeros((size, ref.shape[1]), jnp.bfloat16)
+                ref[stop:stop + left, :] = jnp.zeros((left, ref.shape[1]), jnp.bfloat16)
     has_before = jnp.where(me > 0, 1.0, 0.0)
     has_after = jnp.where(me < total - 1, 1.0, 0.0)
     small[1].wait()
@@ -268,34 +281,41 @@
             hi_ref[rows, r * h:(r + 1) * h] = high[r * part:(r + 1) * part]
             lo_ref[rows, r * h:(r + 1) * h] = low[r * part:(r + 1) * part]
 
-    sent = []
-    waiting = {}
+    stages = {}
+
+    def every(body):
+        if total <= 64:
+            for d in sorted(range(1, total), key=lambda d: -min(d, total - d)):
+                body(d)
+        else:
+            pl.loop(1, total)(body)
+
+    def move(g, stage, src, dst, peer):
+        send_sem, recv_sem = ((s1, r1), (s2, r2))[stage]
+        return pltpu.make_async_remote_copy(
+            src_ref=src, dst_ref=dst, send_sem=send_sem.at[g], recv_sem=recv_sem.at[g],
+            device_id=(lax.div(peer, tiles), lax.rem(peer, tiles)), device_id_type=MESH)
+
+    def all_of(g, stage):
+        ref = bufs[g][1 + stage].at[pl.ds(0, total - 1)]
+        return move(g, stage, ref, ref, after)
 
     def launch(g, stage):
-        mine, near, far, whole = bufs[g]
-        copies = []
-        for d in range(1, ccds if stage == 2 else tiles):
-            i = d - 1
-            if stage == 1:
-                peer = lax.rem(t + d, tiles)
-                copy = pltpu.make_async_remote_copy(
-                    src_ref=mine.at[peer], dst_ref=near.at[i], send_sem=s1.at[g, i], recv_sem=r1.at[g, i],
-                    device_id=(c, peer), device_id_type=MESH)
-            elif stage == 2:
-                copy = pltpu.make_async_remote_copy(
-                    src_ref=far.at[c], dst_ref=far.at[c], send_sem=s2.at[g, i], recv_sem=r2.at[g, i],
-                    device_id=(lax.rem(c + d, ccds), t), device_id_type=MESH)
+        mine, near, whole = bufs[g]
+
+        def body(d):
+            peer = lax.rem(me + d, total)
+            if stage == 0:
+                move(g, 0, mine.at[peer], near.at[d - 1], peer).start()
             else:
-                copy = pltpu.make_async_remote_copy(
-                    src_ref=whole.at[t], dst_ref=whole.at[t], send_sem=s3.at[g, i], recv_sem=r3.at[g, i],
-                    device_id=(c, lax.rem(t + d, tiles)), device_id_type=MESH)
-            copy.start()
-            copies.append(copy)
-        sent.extend(copies)
-        waiting[g] = (stage, copies)
+                move(g, 1, whole.at[me], whole.at[me], peer).start()
+
+        every(body)
+        stages[g] = stage
 
     def gram(g):
-        first, stop = g * size, (g + 1) * size
+        first, stop = group_rows(exposures, g)
+        size = stop - first
         wide = (first // LANES + 1) * LANES
         some = jnp.concatenate([hi_ref[first:stop, :], lo_ref[first:stop, :]], axis=0)
         value = product(some, hi_ref[:wide, :], (1, 1)) + product(some, lo_ref[:wide, :], (1, 1))
@@ -303,74 +323,77 @@
         packed = jnp.concatenate([value[:, w:w + LANES] for w in range(0, wide, LANES)], axis=0)
         mine = bufs[g][0]
         share = mine.shape[1]
+        if g == 0:
+            pl.semaphore_wait(ready, ccds - 1)
         for i in range(packed.shape[0] // share):
             mine[i] = packed[i * share:(i + 1) * share]
-        launch(g, 1)
+        launch(g, 0)
 
     def advance(g):
-        mine, near, far, whole = bufs[g]
-        stage, copies = waiting[g]
-        for copy in copies:
-            copy.wait_recv()
-        if stage == 1:
-            value = mine[t]
-            for d in range(1, tiles):
-                value = value + near[d - 1]
-            far[c] = value
-            launch(g, 2)
-        elif stage == 2:
-            value = far[0]
-            for i in range(1, ccds):
-                value = value + far[i]
-            whole[t] = value
-            launch(g, 3)
+        mine, near, whole = bufs[g]
+        all_of(g, stages[g]).wait_recv()
+        if stages[g] == 0:
+            whole[me] = mine[me] + jnp.sum(near[:total - 1], axis=0)
+            launch(g, 1)
+
+    def gathered(g, ref):
+        whole = bufs[g][2]
+        tall, share = shares(exposures, total, g)
+        for i in range(tall // share):
+            ref[i * share:(i + 1) * share, :] = whole[i]
+        return tall
 
     def factor(g):
-        whole = bufs[g][3]
-        value = whole[...].reshape(-1, LANES) * scale
-        tiles_in = [value[w * size:(w + 1) * size] for w in range(g * size // LANES + 1)]
-        rows = slice(g * size, (g + 1) * size)
-        at, start = divmod(g * size, LANES)
-        low, spread, block = panel(tiles_in, g * size, x_ref[:(at + 1) * LANES, :(at + 1) * LANES], lows)
+        value = flat[0, :gathered(g, flat.at[0]), :] * scale
+        first, stop = group_rows(exposures, g)
+        size, rows = stop - first, slice(first, stop)
+        at, start = divmod(first, LANES)
+        tiles_in = [value[w * size:(w + 1) * size] for w in range(at + 1)]
+        low, spread, block = panel(tiles_in, first, x_ref[:(at + 1) * LANES, :(at + 1) * LANES], lows)
         lane = lax.broadcasted_iota(jnp.int32, block.shape, 1)
         live = [block if low is None else jnp.where(lane < start, -spread[:, at * LANES:], block)]
         if at:
             live = [-spread[:, w * LANES:(w + 1) * LANES] for w in range(at)] + live
         fill = []
         if g:
-            last = slice((g - 1) * size, g * size)
-            deep = ((g - 1) * size // LANES + 1) * LANES
-            both = jnp.concatenate(split(x_ref[last, :deep]), axis=0)
-            fill = pieces(both, hi_ref, lo_ref, functools.partial(spread_rows, out32, tile_rows, size))
-        eliminate(live, g * size, rows_ref, fill)
+            last = group_rows(exposures, g - 1)
+            deep = (last[0] // LANES + 1) * LANES
+            both = jnp.concatenate(split(x_ref[last[0]:last[1], :deep]), axis=0)
+            fill = pieces(both, hi_ref, lo_ref, functools.partial(spread_rows, out32, tile_rows, last[1] - last[0]))
+        eliminate(live, first, rows_ref, fill)
         cut = slice(at * LANES, (at + 1) * LANES)
-        upper, lower = triangles(rows_ref[:, cut], start)
+        upper, lower = triangles(rows_ref[:size, cut], start)
         x_ref[rows, cut] = lower
         f_ref[rows, cut] = upper if low is None else jnp.where(lane < start, low[:, cut], upper)
         if at:
-            x_ref[rows, :at * LANES] = rows_ref[:, :at * LANES]
+            x_ref[rows, :at * LANES] = rows_ref[:size, :at * LANES]
             f_ref[rows, :at * LANES] = low[:, :at * LANES]
         if g:
-            early_ref[(g - 1) * size * tile_rows:g * size * tile_rows, :] = out32[...].astype(jnp.bfloat16)
-
-    per = CHUNKS // GROUPS
+            tall = (last[1] - last[0]) * tile_rows
+            early_ref[last[0] * tile_rows:last[1] * tile_rows, :] = out32[:tall, :].astype(jnp.bfloat16)
+
     for k in range(CHUNKS):
         for copy in moves[k]:
             copy.wait_recv()
-        if k % per == per - 1:
-            for g in range(max(0, k // per - 3), k // per):
-                advance(g)
+        for g in SLOTS.get(k, ()):
+            advance(g)
         smooth(k)
-        if k % per == per - 1:
-            gram(k // per)
+        if k + 1 in BOUNDS:
+            gram(BOUNDS.index(k + 1) - 1)
         if k + AHEAD < CHUNKS:
             send(k + AHEAD)
-    for n in range(3):
-        factor(GROUPS - 4 + n)
-        for g in range(GROUPS - 1, GROUPS - 4 + n, -1):
-            advance(g)
-    g_ref[...] = bufs[GROUPS - 1][3][...]
-    for copy in sum(moves, []) + sent:
+        if k == FIRST:
+            factor(0)
+    for order, g in TAIL:
+        for i in order:
+            advance(i)
+        if g is not None:
+            factor(g)
+    gathered(GROUPS - 1, g_ref)
+    for g in range(GROUPS):
+        for stage in range(2):
+            all_of(g, stage).wait_send()
+    for copy in sum(moves, []):
         copy.wait_send()
 
 
@@ -378,22 +401,23 @@
     ccds, tiles = lax.axis_size("ccd"), lax.axis_size("tile")
     exposures, tile_rows, _ = frames.shape
     pixels = tile_rows * LANES
-    part, size = exposures // CHUNKS, exposures // GROUPS
+    part = exposures // CHUNKS
     span = part * tile_rows
+    size = max(stop - first for first, stop in (group_rows(exposures, g) for g in range(GROUPS)))
+    early = group_rows(exposures, GROUPS - 2)[0]
     dma = pltpu.SemaphoreType.DMA
     vm = pl.BlockSpec(memory_space=pltpu.VMEM)
     hbm = pl.BlockSpec(memory_space=pl.ANY)
     split_shape = pltpu.VMEM((exposures, pixels), jnp.bfloat16)
     square = pltpu.VMEM((exposures, exposures), jnp.float32)
-    share = [shares(size, tiles, g) for g in range(GROUPS)]
+    share = [shares(exposures, ccds * tiles, g) for g in range(GROUPS)]
     reduce = []
     for g in range(GROUPS):
-        for n in (tiles, tiles - 1, ccds, tiles):
-            reduce.append(pltpu.VMEM((n, share[g], LANES), jnp.float32))
+        reduce += [pltpu.VMEM((ccds * tiles, share[g][1], LANES), jnp.float32)] * 3
     return pl.pallas_call(
         functools.partial(exchange_kernel, ccds, tiles, pixel_total),
-        out_shape=(split_shape, split_shape, pltpu.VMEM((tiles, share[-1], LANES), jnp.float32), square, square,
-                   pltpu.VMEM(((GROUPS - 2) * size * tile_rows, LANES), jnp.bfloat16)),
+        out_shape=(split_shape, split_shape, pltpu.VMEM((share[-1][0], LANES), jnp.float32), square, square,
+                   pltpu.VMEM((early * tile_rows, LANES), jnp.bfloat16)),
         in_specs=[hbm] * 4,
         out_specs=(vm,) * 6,
         scratch_shapes=[
@@ -411,9 +435,8 @@
             *reduce,
             dma((CHUNKS,)), dma((CHUNKS,)), dma((2,)),
             dma((2, CHUNKS)), dma((2, CHUNKS)),
-            dma((GROUPS, tiles - 1)), dma((GROUPS, tiles - 1)),
-            dma((GROUPS, ccds - 1)), dma((GROUPS, ccds - 1)),
-            dma((GROUPS, tiles - 1)), dma((GROUPS, tiles - 1)),
+            dma((GROUPS,)), dma((GROUPS,)), dma((GROUPS,)), dma((GROUPS,)),
+            pltpu.SemaphoreType.REGULAR,
         ],
         compiler_params=pltpu.CompilerParams(collective_id=0, has_side_effects=True, vmem_limit_bytes=VMEM),
     )(*(pltpu.with_memory_space_constraint(x, pltpu.HBM) for x in (frames, source_mask, good_pixels, weights)))
@@ -423,9 +446,8 @@
                  lows, rows_ref, out32, packed, rest_hi, rest_lo, factor, sems):
     exposures, pixels = hi_ref.shape
     tile_rows = pixels // LANES
-    size = exposures // GROUPS
-    span = size * tile_rows
-    first = exposures - size
+    before, first = group_rows(exposures, GROUPS - 2)
+    size, prior = exposures - first, first - before
     at, start = divmod(first, LANES)
     copies = []
 
@@ -436,44 +458,60 @@
 
     out(early_ref, b_hbm.at[pl.ds(0, early_ref.shape[0])])
     lows[...] = jnp.zeros(lows.shape, jnp.float32)
-    value = g_ref[...].reshape(-1, LANES) * (1.0 / pixel_total)
+    value = g_ref[...] * (1.0 / pixel_total)
     low, spread, block = panel([value[w * size:(w + 1) * size] for w in range(at + 1)], first, x_ref[...], lows)
     row = first + lax.broadcasted_iota(jnp.int32, (size, exposures), 0)
     col = lax.broadcasted_iota(jnp.int32, (size, exposures), 1)
     rest = jnp.where(col < first, -spread, jnp.where(col == row, 1.0, 0.0))
-    xh, xl = split(x_ref[first - size:first, :])
+    xh, xl = split(x_ref[before:first, :])
     rh, rl = split(rest)
     both = jnp.concatenate([xh, rh, xl, rl], axis=0)
 
     def keep(cut, value):
-        spread_rows(out32, tile_rows, size, cut, value)
-        high, small = split(value[size:])
+        spread_rows(out32, tile_rows, prior, cut, value)
+        high, small = split(value[prior:])
         rest_hi[:, cut:cut + 2 * LANES] = high
         rest_lo[:, cut:cut + 2 * LANES] = small
 
-    eliminate([block], start, rows_ref, pieces(both, hi_ref, lo_ref, keep))
+    def rows_out(top, stop):
+        tall = (stop - top) * tile_rows
+        here = pl.ds((top - before) * tile_rows, tall)
+        packed[here, :] = out32[:tall, :].astype(jnp.bfloat16)
+        out(packed.at[here], b_hbm.at[pl.ds(top * tile_rows, tall)])
+
+    def upper_rows():
+        whole = jnp.concatenate([f_ref[:first, :], jnp.where(col < first, low, 0.0)], axis=0)
+        down = lax.broadcasted_iota(jnp.int32, (exposures, exposures), 0)
+        over = lax.broadcasted_iota(jnp.int32, (exposures, exposures), 1)
+        same = over < 0
+        for g in range(GROUPS - 1):
+            a, b = group_rows(exposures, g)
+            ranges = [jnp.logical_and(i >= a, i < b) for i in (down, over)]
+            same = jnp.logical_or(same, jnp.logical_and(*ranges))
+        both_sides = jnp.where(same, whole, 0.0) + jnp.where(jnp.logical_or(same, over > down), 0.0, whole).T
+        factor[:first, :] = both_sides[:first]
+        out(factor.at[pl.ds(0, first)], o_hbm.at[pl.ds(0, first)])
+
+    fill = [upper_rows] + pieces(both, hi_ref, lo_ref, keep)
+    eliminate([block], start, rows_ref, fill)
     upper, lower = triangles(rows_ref[...], start)
-    packed[:span, :] = out32[...].astype(jnp.bfloat16)
-    out(packed.at[pl.ds(0, span)], b_hbm.at[pl.ds((exposures - 2 * size) * tile_rows, span)])
+    rows_out(before, first)
+    if at:
+        factor[first:, :at * LANES] = jnp.zeros((size, at * LANES), jnp.float32)
+    factor[first:, at * LANES:] = upper
+    out(factor.at[pl.ds(first, size)], o_hbm.at[pl.ds(first, size)])
     both = jnp.concatenate(split(lower[:, start:start + size]), axis=0)
     for piece in pieces(both, rest_hi, rest_lo, functools.partial(spread_rows, out32, tile_rows, size)):
         piece()
-    packed[span:, :] = out32[...].astype(jnp.bfloat16)
-    out(packed.at[pl.ds(span, span)], b_hbm.at[pl.ds(first * tile_rows, span)])
-    whole = jnp.where(col < first, low, jnp.pad(upper, ((0, 0), (at * LANES, 0))) if at else upper)
-    whole = jnp.concatenate([f_ref[:first, :], whole], axis=0)
-    row = lax.broadcasted_iota(jnp.int32, (exposures, exposures), 0) // size
-    col = lax.broadcasted_iota(jnp.int32, (exposures, exposures), 1) // size
-    factor[...] = jnp.where(row == col, whole, 0.0) + jnp.where(col < row, whole, 0.0).T
-    out(factor, o_hbm)
+    rows_out(first, exposures)
     for copy in copies:
         copy.wait()
 
 
 def solve(gram, x, f, early, hi, lo, pixel_total):
     exposures, pixels = hi.shape
-    size = exposures // GROUPS
-    span = size * pixels // LANES
+    before, first = group_rows(exposures, GROUPS - 2)
+    size, tile_rows = exposures - first, pixels // LANES
     vm = pl.BlockSpec(memory_space=pltpu.VMEM)
     hbm = pl.BlockSpec(memory_space=pl.ANY)
     square = (exposures, exposures)
@@ -487,12 +525,12 @@
         scratch_shapes=[
             pltpu.VMEM(square, jnp.float32),
             pltpu.VMEM((size, LANES), jnp.float32),
-            pltpu.VMEM((span, LANES), jnp.float32),
-            pltpu.VMEM((2 * span, LANES), jnp.bfloat16),
+            pltpu.VMEM((max(size, first - before) * tile_rows, LANES), jnp.float32),
+            pltpu.VMEM(((exposures - before) * tile_rows, LANES), jnp.bfloat16),
             pltpu.VMEM((size, pixels), jnp.bfloat16),
             pltpu.VMEM((size, pixels), jnp.bfloat16),
             pltpu.VMEM(square, jnp.float32),
-            pltpu.SemaphoreType.DMA((4,)),
+            pltpu.SemaphoreType.DMA((5,)),
         ],
         compiler_params=pltpu.CompilerParams(vmem_limit_bytes=VMEM),
     )(*given)

time: 52.3 us -> 50.5 us (0.966)
  Pallas kernels: 51.3 us -> 49.6 us
    pallas_call x1, Pallas kernels: 4.53 us -> 2.91 us  [solve(): pl.pallas_call(functools.partial(solve_kernel, pixel_total), out_shape=(j...]
where the time goes in v4:
time: 50.5 us; the launch traced here: 50.4 us
  Pallas kernels  49.6 us (98%)
  between operations  0.8 us (2%)
    pallas_call x1, Pallas kernels, exchange(): pl.pallas_call(functools.partial(exchange_kernel, ccds, tiles, pixel_tota...  46.7 us
    pallas_call x1, Pallas kernels, solve(): pl.pallas_call(functools.partial(solve_kernel, pixel_total), out_shape=(j...  2.91 us

profile of v4, /device:TPU:0, one launch (start us, length us, event | category | flops | bytes accessed | tf_op | source)
XLA Modules:
  0.0 50.4 jit_solution(7122567788952941911)
XLA Ops:
  0.6 46.7 %shard_map.59 = (bf16[256,2048]{1,0:T(8,128)(2,1)S(1)}, bf16[256,2048]{1,0:T(8,128)(2,1)S(1)}, f32[64,128]{1,0:T(8,128)S(1)}, f32[256,256]{1,0:T(8,128)S(1)}, f3...) custom-call(bf16[256,16,128]{2,1,0:T(8,128)(2,1)} %frame_hbm.1, s32[256,16,128]{2,1,0:T(8,128)} %mask_hbm.1, ...), custom_call_target="tpu_custom_call" | custom-call | tf_op jit(solution)/shard_map/pallas_call | solution.py:417
  47.3 2.9 %shard_map.60 = (f32[256,256]{1,0:T(8,128)}, bf16[4096,128]{1,0:T(8,128)(2,1)}) custom-call(f32[64,128]{1,0:T(8,128)S(1)} %get-tuple-element.10.g_ref, f32[256,256]{1,0:T(8,128)S(1)} %get-tuple-element.11.x_ref, f32[256,256]{1,0:T(8,128)S(1)} %get-tuple-element.12.f_ref, bf16[3072,128]{1,0:T(8,128)(2,1)S(1)} %get-tuple-element.13.early_ref, ...), custom_call_target="tpu_custom_call" | custom-call | tf_op jit(solution)/shard_map/pallas_call | solution.py:520

commit v5 on v4

--- a/solution.py
+++ b/solution.py
@@ -19,6 +19,8 @@
 AHEAD = 4
 SLOTS = {8: (0,), 12: (1,), 13: (0,), 15: (2,)}
 FIRST = 13
+BESIDE = {1: 0, 3: 2}
+BEHIND = (1,)
 TAIL = (((3, 1), 1), ((4, 2), 2), ((3,), 3), ((4,), None))
 VMEM = 40 << 20
 
@@ -285,7 +287,7 @@
 
     def every(body):
         if total <= 64:
-            for d in sorted(range(1, total), key=lambda d: -min(d, total - d)):
+            for d in range(1, total):
                 body(d)
         else:
             pl.loop(1, total)(body)
@@ -333,7 +335,10 @@
         mine, near, whole = bufs[g]
         all_of(g, stages[g]).wait_recv()
         if stages[g] == 0:
-            whole[me] = mine[me] + jnp.sum(near[:total - 1], axis=0)
+            parts = [mine[me]] + [near[i] for i in range(total - 1)] if total <= 64 else [mine[me] + jnp.sum(near[:total - 1], axis=0)]
+            while len(parts) > 1:
+                parts = [a + b for a, b in zip(parts[::2], parts[1::2])] + parts[len(parts) // 2 * 2:]
+            whole[me] = parts[0]
             launch(g, 1)
 
     def gathered(g, ref):
@@ -342,6 +347,15 @@
         for i in range(tall // share):
             ref[i * share:(i + 1) * share, :] = whole[i]
         return tall
+
+    def basis(g):
+        first, stop = group_rows(exposures, g)
+        both = jnp.concatenate(split(x_ref[first:stop, :(first // LANES + 1) * LANES]), axis=0)
+        return pieces(both, hi_ref, lo_ref, functools.partial(spread_rows, out32, tile_rows, stop - first))
+
+    def keep(g):
+        first, stop = group_rows(exposures, g)
+        early_ref[first * tile_rows:stop * tile_rows, :] = out32[:(stop - first) * tile_rows, :].astype(jnp.bfloat16)
 
     def factor(g):
         value = flat[0, :gathered(g, flat.at[0]), :] * scale
@@ -354,13 +368,8 @@
         live = [block if low is None else jnp.where(lane < start, -spread[:, at * LANES:], block)]
         if at:
             live = [-spread[:, w * LANES:(w + 1) * LANES] for w in range(at)] + live
-        fill = []
-        if g:
-            last = group_rows(exposures, g - 1)
-            deep = (last[0] // LANES + 1) * LANES
-            both = jnp.concatenate(split(x_ref[last[0]:last[1], :deep]), axis=0)
-            fill = pieces(both, hi_ref, lo_ref, functools.partial(spread_rows, out32, tile_rows, last[1] - last[0]))
-        eliminate(live, first, rows_ref, fill)
+        beside = BESIDE.get(g)
+        eliminate(live, first, rows_ref, () if beside is None else basis(beside))
         cut = slice(at * LANES, (at + 1) * LANES)
         upper, lower = triangles(rows_ref[:size, cut], start)
         x_ref[rows, cut] = lower
@@ -368,9 +377,12 @@
         if at:
             x_ref[rows, :at * LANES] = rows_ref[:size, :at * LANES]
             f_ref[rows, :at * LANES] = low[:, :at * LANES]
-        if g:
-            tall = (last[1] - last[0]) * tile_rows
-            early_ref[last[0] * tile_rows:last[1] * tile_rows, :] = out32[:tall, :].astype(jnp.bfloat16)
+        if beside is not None:
+            keep(beside)
+        if g in BEHIND:
+            for piece in basis(g):
+                piece()
+            keep(g)
 
     for k in range(CHUNKS):
         for copy in moves[k]:

time: 50.5 us -> 50.2 us (level)
  no operation moved by 1% of the time
where the time goes in v5:
time: 50.2 us; the launch traced here: 50.1 us
  Pallas kernels  49.3 us (98%)
  between operations  0.8 us (2%)
    pallas_call x1, Pallas kernels, exchange(): pl.pallas_call(functools.partial(exchange_kernel, ccds, tiles, pixel_tota...  46.3 us
    pallas_call x1, Pallas kernels, solve(): pl.pallas_call(functools.partial(solve_kernel, pixel_total), out_shape=(j...  2.91 us

profile of v5, /device:TPU:0, one launch (start us, length us, event | category | flops | bytes accessed | tf_op | source)
XLA Modules:
  0.0 50.1 jit_solution(8776884880229748486)
XLA Ops:
  0.6 46.3 %shard_map.59 = (bf16[256,2048]{1,0:T(8,128)(2,1)S(1)}, bf16[256,2048]{1,0:T(8,128)(2,1)S(1)}, f32[64,128]{1,0:T(8,128)S(1)}, f32[256,256]{1,0:T(8,128)S(1)}, f3...) custom-call(bf16[256,16,128]{2,1,0:T(8,128)(2,1)} %frame_hbm.1, s32[256,16,128]{2,1,0:T(8,128)} %mask_hbm.1, ...), custom_call_target="tpu_custom_call" | custom-call | tf_op jit(solution)/shard_map/pallas_call | solution.py:429
  47.0 2.9 %shard_map.60 = (f32[256,256]{1,0:T(8,128)}, bf16[4096,128]{1,0:T(8,128)(2,1)}) custom-call(f32[64,128]{1,0:T(8,128)S(1)} %get-tuple-element.10.g_ref, f32[256,256]{1,0:T(8,128)S(1)} %get-tuple-element.11.x_ref, f32[256,256]{1,0:T(8,128)S(1)} %get-tuple-element.12.f_ref, bf16[3072,128]{1,0:T(8,128)(2,1)S(1)} %get-tuple-element.13.early_ref, ...), custom_call_target="tpu_custom_call" | custom-call | tf_op jit(solution)/shard_map/pallas_call | solution.py:532
